TPU v7x, 32 devices: a whole 2x2x4 slice. The times are simulated.
32 devices in a mesh: gx: 4 (over z), gy: 2 (over y), gz: 4 (over x, core).
Axes of the slice: x: 2, y: 2, z: 4, core: 2. Of those that a mesh axis runs over, the one named last changes fastest.
Arguments:
- adjoint_guess: float32 [2, 20, 128, 1024], P(None, 'gz', 'gy', 'gx'), may hold values from -6 to 6
- viscosity: float32 [20, 128, 1024], P('gz', 'gy', 'gx'), may hold values from 0.2 to 2
- friction: float32 [128, 1024], P('gy', 'gx'), may hold values from 0.2 to 5
- base_velocity: float32 [2, 128, 1024], P(None, 'gy', 'gx'), may hold values from -6 to 6
- surface_slope: float32 [2, 128, 1024], P(None, 'gy', 'gx'), may hold values from -6 to 6
- ice_mask: int32 [128, 1024], P('gy', 'gx'), may hold values 0 or 1
- pixel_misfit: float32 [524288], P(('gx', 'gy', 'gz')), may hold values from -6 to 6
- pixel_look: float32 [524288], P(('gx', 'gy', 'gz')), may hold values from -3.140625 to 3.140625
- pixel_tile: int32 [524288, 1], P(('gx', 'gy', 'gz')), may hold values from 0 to 7; in each aligned block of 16384 rows (0 to 16383, 16384 to 32767, ...) at most 4096 rows name the same one
- pixel_cell: int32 [524288], P(('gx', 'gy', 'gz')), may hold values from 0 to 16383
- pixel_count: int32 [32], P(('gx', 'gy', 'gz')), may hold values from 1 to 16384, 393216 in all
Outputs:
- adjoint: float32 [2, 20, 128, 1024], P(None, 'gz', 'gy', 'gx')
- sensitivity_maps: float32 [2, 128, 1024], P(None, ('gy', 'gz'), 'gx')
Inputs may be any that keep to these rules, and one draw needn't show every extreme that they name: `pixel_tile`: among the rows of one device no tile is named more than 4096 times, a bound that some block reaches. `pixel_count`: rows of a device from its count on are padding.
All inputs are finite; a program needn't handle non-finite values. No bound on the sum of `ice_mask` on one device may be relied on, other than what follows from the above.
Results may differ from a plain program's by a relative error of at most 0.00002.
Values sent between devices are 32-bit elements; how exact they have to be, the bound alone decides.
A program may use at most 128 MiB of HBM per device.

v0:
```python
import jax
import jax.numpy as jnp
from jax import lax
from jax.sharding import PartitionSpec as P

ITERS = 2


OMEGA = 0.6
VERTICAL = 4.0


def padded_2(block, sides, width):
    for axis, dim in sides:
        count = lax.axis_size(axis)
        forward = [(i, i + 1) for i in range(count - 1)]
        backward = [(target, source) for source, target in forward]
        low = lax.ppermute(
            lax.slice_in_dim(block, block.shape[dim] - width, None, axis=dim), axis, forward
        )
        high = lax.ppermute(lax.slice_in_dim(block, 0, width, axis=dim), axis, backward)
        block = jnp.concatenate([low, block, high], axis=dim)
    return block


def box_apply(padded, visc_pad, mask_east, mask_north, mask_upper):
    first = padded[0]
    second = padded[1]
    base_a = first[:-1, :-1, :-1]
    base_b = second[:-1, :-1, :-1]
    east_a = (first[:-1, :-1, 1:] - base_a) * mask_east
    east_b = (second[:-1, :-1, 1:] - base_b) * mask_east
    north_a = (first[:-1, 1:, :-1] - base_a) * mask_north
    north_b = (second[:-1, 1:, :-1] - base_b) * mask_north
    upper_a = (first[1:, :-1, :-1] - base_a) * mask_upper
    upper_b = (second[1:, :-1, :-1] - base_b) * mask_upper
    visc_box = visc_pad[:-1, :-1, :-1]
    along_x = visc_box * (4.0 * east_a + 2.0 * north_b) * mask_east
    along_y = visc_box * (4.0 * north_b + 2.0 * east_a) * mask_north
    shear = visc_box * (north_a + east_b)
    shear_x = shear * mask_east
    shear_y = shear * mask_north
    vert_a = VERTICAL * visc_box * upper_a
    vert_b = VERTICAL * visc_box * upper_b
    result_a = (
        along_x[1:, 1:, :-1]
        - along_x[1:, 1:, 1:]
        + (shear_y[1:, :-1, 1:] - shear_y[1:, 1:, 1:])
        + (vert_a[:-1, 1:, 1:] - vert_a[1:, 1:, 1:])
    )
    result_b = (
        along_y[1:, :-1, 1:]
        - along_y[1:, 1:, 1:]
        + (shear_x[1:, 1:, :-1] - shear_x[1:, 1:, 1:])
        + (vert_b[:-1, 1:, 1:] - vert_b[1:, 1:, 1:])
    )
    return jnp.stack([result_a, result_b])


def body(
    adjoint_guess,
    viscosity,
    friction,
    base_velocity,
    surface_slope,
    ice_mask,
    pixel_misfit,
    pixel_look,
    pixel_tile,
    pixel_cell,
    pixel_count,
):
    layer_local = adjoint_guess.shape[1]
    rows_local = adjoint_guess.shape[2]
    cols_local = adjoint_guess.shape[3]
    count_x = lax.axis_size("gx")
    count_y = lax.axis_size("gy")
    count_z = lax.axis_size("gz")
    layer_total = layer_local * count_z
    full_x = cols_local * count_x
    full_y = rows_local * count_y
    tile_total = count_x * count_y
    per_device = pixel_misfit.shape[0]
    capacity = 2 * per_device // tile_total
    mask_float = ice_mask.astype(jnp.float32)
    live = jnp.arange(per_device, dtype=jnp.int32) < pixel_count[0]
    values = jnp.where(live, pixel_misfit, jnp.float32(0.0))
    dest_tile = pixel_tile[:, 0]
    one_hot = (dest_tile[:, None] == jnp.arange(tile_total, dtype=jnp.int32)[None, :]).astype(
        jnp.int32
    )
    running = jnp.cumsum(one_hot, axis=0)
    slot_index = jnp.sum(one_hot * running, axis=1) - 1
    position = dest_tile * capacity + slot_index
    payload = jnp.stack(
        [values * jnp.cos(pixel_look), values * jnp.sin(pixel_look), pixel_cell.astype(jnp.float32)]
    )
    outbox = jnp.zeros((3, tile_total * capacity), jnp.float32).at[:, position].set(payload)
    inbox = lax.all_to_all(
        outbox.reshape(3, tile_total, capacity),
        ("gx", "gy"),
        split_axis=1,
        concat_axis=1,
        tiled=True,
    )
    received = inbox.reshape(3, tile_total * capacity)
    cell_ids = received[2].astype(jnp.int32)
    forcing = jnp.zeros((2, rows_local * cols_local), jnp.float32).at[:, cell_ids].add(received[:2])
    forcing = forcing.reshape(2, rows_local, cols_local)
    forcing = lax.psum(forcing, "gz") * mask_float[None]
    layer_ids = lax.axis_index("gz") * layer_local + jnp.arange(layer_local, dtype=jnp.int32)
    bottom = (layer_ids == 0).astype(jnp.float32)[:, None, None]
    top = (layer_ids == layer_total - 1).astype(jnp.float32)[:, None, None]
    rhs = forcing[:, None, :, :] * top[None]
    basal = friction[None] * bottom
    damping = OMEGA / (18.0 * viscosity + basal)
    east_ids = lax.axis_index("gx") * cols_local + jnp.arange(cols_local + 1, dtype=jnp.int32) - 1
    north_ids = lax.axis_index("gy") * rows_local + jnp.arange(rows_local + 1, dtype=jnp.int32) - 1
    upper_ids = (
        lax.axis_index("gz") * layer_local + jnp.arange(layer_local + 1, dtype=jnp.int32) - 1
    )
    mask_east = (east_ids + 1 < full_x).astype(jnp.float32)[None, None, :]
    mask_north = (north_ids + 1 < full_y).astype(jnp.float32)[None, :, None]
    mask_upper = (upper_ids + 1 < layer_total).astype(jnp.float32)[:, None, None]
    adjoint = adjoint_guess
    for sweep in range(ITERS):
        stacked = jnp.concatenate([adjoint, viscosity[None]], axis=0)
        rims = padded_2(stacked, (("gx", 3), ("gy", 2), ("gz", 1)), 1)
        image = (
            box_apply(rims[:2], rims[2], mask_east, mask_north, mask_upper) + basal[None] * adjoint
        )
        adjoint = adjoint + damping[None] * (rhs - image)
    on_base = (lax.axis_index("gz") == 0).astype(jnp.float32)
    fric_term = (
        -on_base
        * mask_float
        * friction
        * (base_velocity[0] * adjoint[0, 0] + base_velocity[1] * adjoint[1, 0])
    )
    drive_term = (
        0.25
        * mask_float
        * jnp.sum(surface_slope[0][None] * adjoint[0] + surface_slope[1][None] * adjoint[1], axis=0)
    )
    maps = lax.psum_scatter(
        jnp.stack([fric_term, drive_term]), "gz", scatter_dimension=1, tiled=True
    )
    return (adjoint, maps)


def solution(mesh):
    return jax.shard_map(
        body,
        mesh=mesh,
        in_specs=(
            P(None, "gz", "gy", "gx"),
            P("gz", "gy", "gx"),
            P("gy", "gx"),
            P(None, "gy", "gx"),
            P(None, "gy", "gx"),
            P("gy", "gx"),
            P(("gx", "gy", "gz")),
            P(("gx", "gy", "gz")),
            P(("gx", "gy", "gz"), None),
            P(("gx", "gy", "gz")),
            P(("gx", "gy", "gz")),
        ),
        out_specs=(P(None, "gz", "gy", "gx"), P(None, ("gy", "gz"), "gx")),
        check_vma=False,
    )
```

profile of v0, /device:TPU:21, one launch (start us, length us, event | category | flops | bytes accessed | tf_op | source)
XLA Modules:
  0.0 576.3 jit_solution(1309384241617030706)
XLA Ops:
  7.2 2.4 fusion.57
  9.5 3.2 collective-permute-start
  17.6 5.1 copy.28
  24.2 47.4 %scatter_custom_fusion = f32[3,32768]{0,1:T(8,128)} fusion(s32[16384]{0:T(1024)S(1)} %bitcast.116, f32[16384,3]{1,0:T(8,128)} %copy.28, f32[]{:T(128)} %constant.26.clone.1), kind=kCustom, calls=%fused_computation.2 | custom fusion | bytes 393728 | tf_op jit(solution)/shard_map/scatter | solution.py:98
  71.6 9.9 %copy.29 = f32[3,8,4096]{2,0,1:T(4,128)} copy(f32[3,8,4096]{0,2,1:T(8,128)} %bitcast.96) | data formatting | bytes 786432 | tf_op jit(solution)/shard_map/reshape | solution.py:100
  81.5 5.7 all-to-all-start
  89.2 4.0 collective-permute-start.3
  94.9 5.9 %collective-permute-start.4 = (f32[3,1,66,258]{3,2,1,0:T(8,128)S(1)}, f32[3,1,66,258]{3,2,1,0:T(8,128)S(1)}, u32[]{:S(2)}, u32[]{:S(2)}) collective-permute-start(f32[3,1,66,258]{3,2,1,0:T(8,128)S(1)} %get-tuple-element.18), channel_id=1, source_target_pairs={{0,1},{1,2},{2,3},{4,5},{5,6},{6,7},{8,9},{9,10},{10,11},{12,13},{... | collective-permute-start | bytes 613016 | tf_op jit(solution)/shard_map/ppermute | solution.py:18
  104.8 4.4 collective-permute-done.5
  114.2 8.3 %copy.30 = f32[32768,2]{1,0:T(8,128)} copy(f32[32768,2]{0,1:T(2,128)S(1)} %bitcast.107) | data formatting | bytes 524288 | tf_op jit(solution)/shard_map/slice | solution.py:108
  122.8 217.4 %scatter_custom_fusion.1 = f32[2,16384]{0,1:T(8,128)} fusion(s32[32768]{0:T(1024)S(1)} %bitcast.115, f32[32768,2]{1,0:T(8,128)} %copy.30, f32[]{:T(128)} %constant.26.clone.1), kind=kCustom, calls=%fused_computation.5 | custom fusion | flops 65536 | bytes 131584 | tf_op jit(solution)/shard_map/scatter-add | solution.py:108
  340.2 3.4 fusion.69
  343.7 147.8 %all-reduce.2.cloned.1.call-done = f32[2,64,256]{0,2,1:T(8,128)} async-done(((f32[2,64,256]{0,2,1:T(8,128)}), f32[2,64,256]{0,2,1:T(8,128)}) %all-reduce.2.cloned.1.call-update) | async-done | bytes 131088 | tf_op jit(solution)/shard_map/psum | solution.py:110
  491.4 7.9 %broadcast_multiply_fusion = f32[2,64,256]{0,2,1:T(8,128)} fusion(f32[2,64,256]{0,2,1:T(8,128)} %all-reduce.2.cloned.1.call-done, f32[64,256]{1,0:T(8,128)S(1)} %convert_element_type.67), kind=kLoop, calls=%fused_computation.4 | loop fusion | flops 32768 | bytes 327680 | tf_op jit(solution)/shard_map/mul | solution.py:110
  499.3 5.2 copy.31
  505.0 3.1 collective-permute-start.6
  508.1 2.2 collective-permute-start.7
  510.3 8.4 %collective-permute-done.6 = f32[3,5,64,1]{3,2,1,0:T(8,128)S(1)} collective-permute-done((f32[3,5,64,1]{3,2,1,0:T(8,128)S(1)}, f32[3,5,64,1]{3,2,1,0:T(8,128)S(1)}, u32[]{:S(2)}, u32[]{:S(2)}) %collective-permute-start.6) | collective-permute-done | bytes 3872 | tf_op jit(solution)/shard_map/ppermute | solution.py:18
  518.6 2.8 collective-permute-done.7
  524.0 5.2 collective-permute-start.9
  531.2 5.8 %collective-permute-start.10 = (f32[3,1,66,258]{3,2,1,0:T(8,128)S(1)}, f32[3,1,66,258]{3,2,1,0:T(8,128)S(1)}, u32[]{:S(2)}, u32[]{:S(2)}) collective-permute-start(f32[3,1,66,258]{3,2,1,0:T(8,128)S(1)} %get-tuple-element.16), channel_id=1, source_target_pairs={{0,1},{1,2},{2,3},{4,5},{5,6},{6,7},{8,9},{9,10},{10,11},{12,13},{... | collective-permute-start | bytes 613016 | tf_op jit(solution)/shard_map/ppermute | solution.py:18
  537.0 2.1 collective-permute-start.11
  541.0 4.4 collective-permute-done.11
  550.7 18.8 %reduce-scatter.2.cloned.1.call-done = f32[2,16,256]{2,1,0:T(8,128)} async-done(((f32[2,64,256]{2,1,0:T(8,128)}), f32[2,16,256]{2,1,0:T(8,128)}) %reduce-scatter.2.cloned.1.call-update) | async-done | bytes 32784 | tf_op jit(solution)/shard_map/reduce_scatter | solution.py:145
  (91 shorter events, 30.4 us)
Async XLA Ops:
  9.5 77.8 %collective-permute-start = (f32[3,5,64,1]{3,2,1,0:T(8,128)}, f32[3,5,64,1]{3,2,1,0:T(8,128)S(1)}, u32[]{:S(2)}, u32[]{:S(2)}) collective-permute-start(f32[3,5,64,1]{3,2,1,0:T(8,128)} %get-tuple-element.26), channel_id=1, source_target_pairs={{0,8},{8,16},{16,24},{1,9},{9,17},{17,25},{2,10},{10,18},{18,26},{... | collective-permute-start | bytes 11528 | tf_op jit(solution)/shard_map/ppermute | solution.py:18
  12.7 74.6 %collective-permute-start.1 = (f32[3,5,64,1]{3,2,1,0:T(8,128)}, f32[3,5,64,1]{3,2,1,0:T(8,128)S(1)}, u32[]{:S(2)}, u32[]{:S(2)}) collective-permute-start(f32[3,5,64,1]{3,2,1,0:T(8,128)} %get-tuple-element.27), channel_id=1, source_target_pairs={{8,0},{16,8},{24,16},{9,1},{17,9},{25,17},{10,2},{18,10},{26,18},{... | collective-permute-start | bytes 11528 | tf_op jit(solution)/shard_map/ppermute | solution.py:21
  17.6 5.1 copy-start.7
  71.6 15.7 %copy-start = (f32[5,64,256]{2,1,0:T(8,128)S(1)}, f32[5,64,256]{2,1,0:T(8,128)}, u32[]{:S(2)}) copy-start(f32[5,64,256]{2,1,0:T(8,128)} %param.12) | copy-start | bytes 983044
  71.6 15.7 %copy-start.1 = (f32[2,5,64,256]{3,2,1,0:T(8,128)S(1)}, f32[2,5,64,256]{3,2,1,0:T(8,128)}, u32[]{:S(2)}) copy-start(f32[2,5,64,256]{3,2,1,0:T(8,128)} %param.11) | copy-start | bytes 1966084
  81.5 11.7 %copy-start.8 = (s32[64,256]{1,0:T(8,128)S(1)}, s32[64,256]{1,0:T(8,128)}, u32[]{:S(2)}) copy-start(s32[64,256]{1,0:T(8,128)} %param.16) | copy-start | bytes 196612
  81.5 32.6 %all-to-all-start = ((f32[3,8,4096]{2,0,1:T(4,128)}), f32[3,8,4096]{2,0,1:T(4,128)S(1)}, u32[]{:S(2)}, u32[]{:S(2)}) async-start(f32[3,8,4096]{2,0,1:T(4,128)} %copy.29), calls=%async_computation | async-start | bytes 1048576 | tf_op jit(solution)/shard_map/all_to_all | solution.py:99
  87.2 404.2 %all-reduce.2.cloned.1.call-start = ((), (), s32[]{:S(2)}) async-start(), calls=%async_computation.2 | async-start | bytes 16777216 | tf_op jit(solution)/shard_map/psum | solution.py:110
  87.9 6.2 %collective-permute-start.2 = (f32[3,5,1,258]{3,2,1,0:T(1,128)S(1)}, f32[3,5,1,258]{3,2,1,0:T(1,128)S(1)}, u32[]{:S(2)}, u32[]{:S(2)}) collective-permute-start(f32[3,5,1,258]{3,2,1,0:T(1,128)S(1)} %get-tuple-element.22), channel_id=1, source_target_pairs={{0,4},{1,5},{2,6},{3,7},{8,12},{9,13},{10,14},{11,15},{16,20},{17,... | collective-permute-start | bytes 46448 | tf_op jit(solution)/shard_map/ppermute | solution.py:18
  89.2 4.9 collective-permute-start.3
  93.3 9.6 %copy-start.9 = (f32[64,256]{1,0:T(8,128)S(1)}, f32[64,256]{1,0:T(8,128)}, u32[]{:S(2)}) copy-start(f32[64,256]{1,0:T(8,128)} %param.13) | copy-start | bytes 196612
  94.9 10.0 %collective-permute-start.4 = (f32[3,1,66,258]{3,2,1,0:T(8,128)S(1)}, f32[3,1,66,258]{3,2,1,0:T(8,128)S(1)}, u32[]{:S(2)}, u32[]{:S(2)}) collective-permute-start(f32[3,1,66,258]{3,2,1,0:T(8,128)S(1)} %get-tuple-element.18), channel_id=1, source_target_pairs={{0,1},{1,2},{2,3},{4,5},{5,6},{6,7},{8,9},{9,10},{10,11},{12,13},{... | collective-permute-start | bytes 613016 | tf_op jit(solution)/shard_map/ppermute | solution.py:18
  100.8 8.4 %collective-permute-start.5 = (f32[3,1,66,258]{3,2,1,0:T(8,128)S(1)}, f32[3,1,66,258]{3,2,1,0:T(8,128)S(1)}, u32[]{:S(2)}, u32[]{:S(2)}) collective-permute-start(f32[3,1,66,258]{3,2,1,0:T(8,128)S(1)} %get-tuple-element.19), channel_id=1, source_target_pairs={{1,0},{2,1},{3,2},{5,4},{6,5},{7,6},{9,8},{10,9},{11,10},{13,12},{... | collective-permute-start | bytes 613016 | tf_op jit(solution)/shard_map/ppermute | solution.py:21
  103.0 401.5 %copy-start.3 = (f32[5,64,256]{2,1,0:T(8,128)}, f32[5,64,256]{2,1,0:T(8,128)S(1)}, u32[]{:S(2)}) copy-start(f32[5,64,256]{2,1,0:T(8,128)S(1)} %get-tuple-element.36) | copy-start | bytes 983044
  103.1 401.5 %copy-start.5 = (f32[5,64,256]{2,1,0:T(8,128)}, f32[5,64,256]{2,1,0:T(8,128)S(1)}, u32[]{:S(2)}) copy-start(f32[5,64,256]{2,1,0:T(8,128)S(1)} %get-tuple-element.37) | copy-start | bytes 983044
  340.2 229.3 %reduce-scatter.2.cloned.1.call-start = ((), (), s32[]{:S(2)}) async-start(), calls=%async_computation.3 | async-start | bytes 163840 | tf_op jit(solution)/shard_map/reduce_scatter | solution.py:145
  505.0 13.7 %collective-permute-start.6 = (f32[3,5,64,1]{3,2,1,0:T(8,128)S(1)}, f32[3,5,64,1]{3,2,1,0:T(8,128)S(1)}, u32[]{:S(2)}, u32[]{:S(2)}) collective-permute-start(f32[3,5,64,1]{3,2,1,0:T(8,128)S(1)} %get-tuple-element.24), channel_id=1, source_target_pairs={{0,8},{8,16},{16,24},{1,9},{9,17},{17,25},{2,10},{10,18},{18,26},{... | collective-permute-start | bytes 11528 | tf_op jit(solution)/shard_map/ppermute | solution.py:18
  508.1 13.4 %collective-permute-start.7 = (f32[3,5,64,1]{3,2,1,0:T(8,128)S(1)}, f32[3,5,64,1]{3,2,1,0:T(8,128)S(1)}, u32[]{:S(2)}, u32[]{:S(2)}) collective-permute-start(f32[3,5,64,1]{3,2,1,0:T(8,128)S(1)} %get-tuple-element.25), channel_id=1, source_target_pairs={{8,0},{16,8},{24,16},{9,1},{17,9},{25,17},{10,2},{18,10},{26,18},{... | collective-permute-start | bytes 11528 | tf_op jit(solution)/shard_map/ppermute | solution.py:21
  522.7 6.5 %collective-permute-start.8 = (f32[3,5,1,258]{3,2,1,0:T(1,128)}, f32[3,5,1,258]{3,2,1,0:T(1,128)}, u32[]{:S(2)}, u32[]{:S(2)}) collective-permute-start(f32[3,5,1,258]{3,2,1,0:T(1,128)} %get-tuple-element.20), channel_id=1, source_target_pairs={{0,4},{1,5},{2,6},{3,7},{8,12},{9,13},{10,14},{11,15},{16,20},{17,... | collective-permute-start | bytes 46448 | tf_op jit(solution)/shard_map/ppermute | solution.py:18
  524.0 5.7 collective-permute-start.9
  529.2 9.9 %copy-start.10 = (f32[2,64,256]{2,1,0:T(8,128)S(1)}, f32[2,64,256]{2,1,0:T(8,128)}, u32[]{:S(2)}) copy-start(f32[2,64,256]{2,1,0:T(8,128)} %param.15) | copy-start | bytes 393220
  531.2 9.8 %collective-permute-start.10 = (f32[3,1,66,258]{3,2,1,0:T(8,128)S(1)}, f32[3,1,66,258]{3,2,1,0:T(8,128)S(1)}, u32[]{:S(2)}, u32[]{:S(2)}) collective-permute-start(f32[3,1,66,258]{3,2,1,0:T(8,128)S(1)} %get-tuple-element.16), channel_id=1, source_target_pairs={{0,1},{1,2},{2,3},{4,5},{5,6},{6,7},{8,9},{9,10},{10,11},{12,13},{... | collective-permute-start | bytes 613016 | tf_op jit(solution)/shard_map/ppermute | solution.py:18
  537.0 8.4 %collective-permute-start.11 = (f32[3,1,66,258]{3,2,1,0:T(8,128)S(1)}, f32[3,1,66,258]{3,2,1,0:T(8,128)S(1)}, u32[]{:S(2)}, u32[]{:S(2)}) collective-permute-start(f32[3,1,66,258]{3,2,1,0:T(8,128)S(1)} %get-tuple-element.17), channel_id=1, source_target_pairs={{1,0},{2,1},{3,2},{5,4},{6,5},{7,6},{9,8},{10,9},{11,10},{13,12},{... | collective-permute-start | bytes 613016 | tf_op jit(solution)/shard_map/ppermute | solution.py:21
  549.4 20.1 %copy-start.2 = (f32[2,5,64,256]{3,2,1,0:T(8,128)}, f32[2,5,64,256]{3,2,1,0:T(8,128)S(1)}, u32[]{:S(2)}) copy-start(f32[2,5,64,256]{3,2,1,0:T(8,128)S(1)} %fusion.51) | copy-start | bytes 1966084
  (3 other events, 3.0 us)
Sparse Core Ops, SparseCore 0:
  340.3 151.1 all-reduce.1
  550.9 18.5 reduce-scatter.1
where the time goes:
time: 579 us; the launch traced here: 576 us
  other arithmetic  248 us (43%)
  waiting for transfers between devices  192 us (33%)
  local copies, waits for them, and re-layouts  78 us (13%)
  starting transfers between devices  44 us (8%)
  between operations  15.2 us (3%)
    scatter-add x1, other arithmetic, body(): jnp.zeros((2, rows_local * cols_local), jnp.float32).at[:, cell_ids]  217 us
    psum x1, waiting for transfers between devices, body(): forcing = lax.psum(forcing, 'gz') * mask_float[None]  148 us
    scatter x1, local copies, waits for them, and re-layouts, body(): jnp.zeros((3, tile_total * capacity), jnp.float32).at[:, position]  47.4 us
    ppermute x6, starting transfers between devices, padded_2(): lax.ppermute(lax.slice_in_dim(block, block.shape[dim] - width, None, axis...  20.6 us
    reduce_scatter x1, waiting for transfers between devices, body(): lax.psum_scatter(jnp.stack([fric_term, drive_term]), 'gz', scatter_dimens...  18.8 us
    ppermute x6, starting transfers between devices, padded_2(): lax.ppermute(lax.slice_in_dim(block, 0, width, axis=dim), axis, backward)  17.7 us
    ppermute x6, waiting for transfers between devices, padded_2(): lax.ppermute(lax.slice_in_dim(block, block.shape[dim] - width, None, axis...  12.8 us
    ppermute x6, waiting for transfers between devices, padded_2(): lax.ppermute(lax.slice_in_dim(block, 0, width, axis=dim), axis, backward)  12.2 us
  transfers between devices with their start and end apart: 15, of which 11 were waited for; matrix products, arithmetic and copies ran while one was open for 13% of the time, Pallas kernels for 0%

commit v1 on v0

--- a/solution.py
+++ b/solution.py
@@ -1,6 +1,10 @@
+import functools
+
 import jax
 import jax.numpy as jnp
 from jax import lax
+from jax.experimental import pallas as pl
+from jax.experimental.pallas import tpu as pltpu
 from jax.sharding import PartitionSpec as P
 
 ITERS = 2
@@ -55,6 +59,69 @@
         + (vert_b[:-1, 1:, 1:] - vert_b[1:, 1:, 1:])
     )
     return jnp.stack([result_a, result_b])
+
+
+def bin_kernel(tiles, rows, cols, fx_ref, fy_ref, tile_ref, cell_ref, out_ref, lhs, rhs):
+    step = pl.program_id(0)
+    depth = fx_ref.shape[1]
+    tile = tile_ref[...]
+    cell = cell_ref[...]
+    col = lax.rem(cell, cols).astype(jnp.float32).astype(jnp.bfloat16)
+    row = lax.div(cell, cols).astype(jnp.float32)
+    fx = fx_ref[...]
+    fy = fy_ref[...]
+    fx_hi = fx.astype(jnp.bfloat16)
+    fy_hi = fy.astype(jnp.bfloat16)
+    fx_lo = (fx - fx_hi.astype(jnp.float32)).astype(jnp.bfloat16)
+    fy_lo = (fy - fy_hi.astype(jnp.float32)).astype(jnp.bfloat16)
+    x_ids = lax.broadcasted_iota(jnp.int32, (cols, depth), 0).astype(jnp.float32).astype(jnp.bfloat16)
+    one = jnp.ones((cols, depth), jnp.bfloat16)
+    rhs[...] = jnp.where(x_ids == col, one, jnp.zeros_like(one))
+    y_ids = lax.broadcasted_iota(jnp.int32, (rows, depth), 0).astype(jnp.float32).astype(jnp.bfloat16)
+    zero = jnp.zeros((rows, depth), jnp.bfloat16)
+    for t in range(tiles):
+        own = jnp.where(tile == t, row, -1.0).astype(jnp.bfloat16)
+        hit = y_ids == own
+        for c, piece in enumerate((fx_hi, fy_hi, fx_lo, fy_lo)):
+            part = c // 2
+            start = (t * 2 + c % 2) * rows
+            lhs[part, start : start + rows, :] = jnp.where(hit, jnp.broadcast_to(piece, (rows, depth)), zero)
+    total = lax.dot_general(
+        lhs[0], rhs[...], (((1,), (1,)), ((), ())), preferred_element_type=jnp.float32
+    ) + lax.dot_general(
+        lhs[1], rhs[...], (((1,), (1,)), ((), ())), preferred_element_type=jnp.float32
+    )
+
+    @pl.when(step == 0)
+    def _():
+        out_ref[...] = total
+
+    @pl.when(step > 0)
+    def _():
+        out_ref[...] += total
+
+
+def bin_pixels(fx, fy, tile, cell, tiles, rows, cols):
+    per_device = fx.shape[0]
+    depth = min(1024, per_device)
+    while depth * tiles * rows * 8 > 24 * 2**20:
+        depth //= 2
+    steps = per_device // depth
+    flat = [value.reshape(steps, 1, depth) for value in (fx, fy, tile, cell)]
+    spec = pl.BlockSpec((None, 1, depth), lambda i: (i, 0, 0))
+    sums = pl.pallas_call(
+        functools.partial(bin_kernel, tiles, rows, cols),
+        grid=(steps,),
+        in_specs=[spec] * 4,
+        out_specs=pl.BlockSpec((tiles * 2 * rows, cols), lambda i: (0, 0)),
+        out_shape=jax.ShapeDtypeStruct((tiles * 2 * rows, cols), jnp.float32),
+        scratch_shapes=[
+            pltpu.VMEM((2, tiles * 2 * rows, depth), jnp.bfloat16),
+            pltpu.VMEM((cols, depth), jnp.bfloat16),
+        ],
+        name="bin_pixels",
+    )(*flat)
+    return sums.reshape(tiles, 2, rows, cols)
 
 
 def body(
@@ -85,27 +152,16 @@
     mask_float = ice_mask.astype(jnp.float32)
     live = jnp.arange(per_device, dtype=jnp.int32) < pixel_count[0]
     values = jnp.where(live, pixel_misfit, jnp.float32(0.0))
-    dest_tile = pixel_tile[:, 0]
-    one_hot = (dest_tile[:, None] == jnp.arange(tile_total, dtype=jnp.int32)[None, :]).astype(
-        jnp.int32
-    )
-    running = jnp.cumsum(one_hot, axis=0)
-    slot_index = jnp.sum(one_hot * running, axis=1) - 1
-    position = dest_tile * capacity + slot_index
-    payload = jnp.stack(
-        [values * jnp.cos(pixel_look), values * jnp.sin(pixel_look), pixel_cell.astype(jnp.float32)]
-    )
-    outbox = jnp.zeros((3, tile_total * capacity), jnp.float32).at[:, position].set(payload)
-    inbox = lax.all_to_all(
-        outbox.reshape(3, tile_total, capacity),
-        ("gx", "gy"),
-        split_axis=1,
-        concat_axis=1,
-        tiled=True,
-    )
-    received = inbox.reshape(3, tile_total * capacity)
-    cell_ids = received[2].astype(jnp.int32)
-    forcing = jnp.zeros((2, rows_local * cols_local), jnp.float32).at[:, cell_ids].add(received[:2])
+    sums = bin_pixels(
+        values * jnp.cos(pixel_look),
+        values * jnp.sin(pixel_look),
+        pixel_tile[:, 0],
+        pixel_cell,
+        tile_total,
+        rows_local,
+        cols_local,
+    )
+    forcing = lax.psum_scatter(sums, ("gx", "gy"), scatter_dimension=0, tiled=True)
     forcing = forcing.reshape(2, rows_local, cols_local)
     forcing = lax.psum(forcing, "gz") * mask_float[None]
     layer_ids = lax.axis_index("gz") * layer_local + jnp.arange(layer_local, dtype=jnp.int32)

time: 579 us -> 212 us (0.37)
  other arithmetic: 248 us -> 19.1 us
  waiting for transfers between devices: 192 us -> 112 us
  local copies, waits for them, and re-layouts: 78 us -> 2.25 us
  Pallas kernels: 0 us -> 24.2 us
  starting transfers between devices: 44 us -> 37.1 us
    scatter-add x1 -> x0, other arithmetic: 217 us -> none  [body(): jnp.zeros((2, rows_local * cols_local), jnp.float32).at[:, cell_ids]]
    psum x1, waiting for transfers between devices: 148 us -> 31.4 us  [body(): forcing = lax.psum(forcing, 'gz') * mask_float[None]]
    scatter x1 -> x0, local copies, waits for them, and re-layouts: 47.4 us -> none  [body(): jnp.zeros((3, tile_total * capacity), jnp.float32).at[:, position]]
    reduce_scatter x0 -> x1, waiting for transfers between devices: none -> 36 us  [body(): lax.psum_scatter(sums, ('gx', 'gy'), scatter_dimension=0, tiled=True)]
    pallas_call x0 -> x1, Pallas kernels: none -> 24.2 us  [bin_pixels(): pl.pallas_call(functools.partial(bin_kernel, tiles, rows, cols), grid=(st...]
    reshape x1 -> x0, local copies, waits for them, and re-layouts: 9.94 us -> none  [body(): outbox.reshape(3, tile_total, capacity)]
    slice x2 -> x0, local copies, waits for them, and re-layouts: 8.38 us -> none  [body(): received[:2]]
    mul x1, other arithmetic: 7.86 us -> 0.92 us  [body(): forcing = lax.psum(forcing, 'gz') * mask_float[None]]
  transfers between devices with their start and end apart: 15 -> 15, of which waited for: 11 -> 11; matrix products, arithmetic and copies ran while one was open for 13% -> 5% of each run, Pallas kernels for 0% -> 12%
where the time goes in v1:
time: 212 us; the launch traced here: 209 us
  waiting for transfers between devices  112 us (53%)
  starting transfers between devices  37.1 us (18%)
  Pallas kernels  24.2 us (11%)
  other arithmetic  19.1 us (9%)
  between operations  14.9 us (7%)
  local copies, waits for them, and re-layouts  2.25 us (1%)
    reduce_scatter x1, waiting for transfers between devices, body(): lax.psum_scatter(sums, ('gx', 'gy'), scatter_dimension=0, tiled=True)  36 us
    psum x1, waiting for transfers between devices, body(): forcing = lax.psum(forcing, 'gz') * mask_float[None]  31.4 us
    pallas_call x1, Pallas kernels, bin_pixels(): pl.pallas_call(functools.partial(bin_kernel, tiles, rows, cols), grid=(st...  24.2 us
    ppermute x6, starting transfers between devices, padded_2(): lax.ppermute(lax.slice_in_dim(block, block.shape[dim] - width, None, axis...  20.7 us
    reduce_scatter x1, waiting for transfers between devices, body(): lax.psum_scatter(jnp.stack([fric_term, drive_term]), 'gz', scatter_dimens...  18.7 us
    ppermute x6, starting transfers between devices, padded_2(): lax.ppermute(lax.slice_in_dim(block, 0, width, axis=dim), axis, backward)  16.2 us
    ppermute x6, waiting for transfers between devices, padded_2(): lax.ppermute(lax.slice_in_dim(block, 0, width, axis=dim), axis, backward)  14 us
    ppermute x6, waiting for transfers between devices, padded_2(): lax.ppermute(lax.slice_in_dim(block, block.shape[dim] - width, None, axis...  11.5 us
  transfers between devices with their start and end apart: 15, of which 11 were waited for; matrix products, arithmetic and copies ran while one was open for 5% of the time, Pallas kernels for 12%

profile of v1, /device:TPU:21, one launch (start us, length us, event | category | flops | bytes accessed | tf_op | source)
XLA Modules:
  0.0 209.2 jit_solution(7752521071766034451)
XLA Ops:
  7.2 1.4 fusion.49
  8.6 3.3 %collective-permute-start = (f32[3,5,64,1]{3,2,1,0:T(8,128)S(1)}, f32[3,5,64,1]{3,2,1,0:T(8,128)S(1)}, u32[]{:S(2)}, u32[]{:S(2)}) collective-permute-start(f32[3,5,64,1]{3,2,1,0:T(8,128)S(1)} %get-tuple-element.26), channel_id=1, source_target_pairs={{0,8},{8,16},{16,24},{1,9},{9,17},{17,25},{2,10},{10,18},{18,26},{... | collective-permute-start | bytes 11528 | tf_op jit(solution)/shard_map/ppermute | solution.py:22
  12.0 2.1 collective-permute-start.1
  15.6 24.2 %bin_pixels.1 = f32[1024,256]{1,0:T(8,128)} custom-call(f32[16,1,1024]{2,1,0:T(1,128)} %bitcast.81, f32[16,1,1024]{2,1,0:T(1,128)} %bitcast.80, s32[16,1,1024]{2,1,0:T(1,128)} %bitcast.83, s32[16,1,1024]{2,1,0:T(1,128)} %bitcast.84), custom_call_target="tpu_custom_call" | custom-call | tf_op jit(solution)/shard_map/bin_pixels/pallas_call | solution.py:112
  41.9 4.0 %collective-permute-start.3 = (f32[3,5,1,258]{3,2,1,0:T(1,128)S(1)}, f32[3,5,1,258]{3,2,1,0:T(1,128)S(1)}, u32[]{:S(2)}, u32[]{:S(2)}) collective-permute-start(f32[3,5,1,258]{3,2,1,0:T(1,128)S(1)} %get-tuple-element.23), channel_id=1, source_target_pairs={{4,0},{5,1},{6,2},{7,3},{12,8},{13,9},{14,10},{15,11},{20,16},{21,... | collective-permute-start | bytes 46448 | tf_op jit(solution)/shard_map/ppermute | solution.py:25
  47.5 5.4 %collective-permute-start.4 = (f32[3,1,66,258]{3,2,1,0:T(8,128)S(1)}, f32[3,1,66,258]{3,2,1,0:T(8,128)S(1)}, u32[]{:S(2)}, u32[]{:S(2)}) collective-permute-start(f32[3,1,66,258]{3,2,1,0:T(8,128)S(1)} %get-tuple-element.18), channel_id=1, source_target_pairs={{0,1},{1,2},{2,3},{4,5},{5,6},{6,7},{8,9},{9,10},{10,11},{12,13},{... | collective-permute-start | bytes 613016 | tf_op jit(solution)/shard_map/ppermute | solution.py:22
  52.9 1.9 collective-permute-start.5
  55.0 1.9 collective-permute-done.4
  57.0 4.8 %collective-permute-done.5 = f32[3,1,66,258]{3,2,1,0:T(8,128)S(1)} collective-permute-done((f32[3,1,66,258]{3,2,1,0:T(8,128)S(1)}, f32[3,1,66,258]{3,2,1,0:T(8,128)S(1)}, u32[]{:S(2)}, u32[]{:S(2)}) %collective-permute-start.5) | collective-permute-done | bytes 204368 | tf_op jit(solution)/shard_map/ppermute | solution.py:25
  62.6 2.0 broadcast_multiply_fusion.1
  66.9 36.0 %reduce-scatter.3.cloned.1.call-done = f32[1,2,64,256]{3,2,1,0:T(8,128)} async-done(((f32[8,2,64,256]{3,2,1,0:T(8,128)}), f32[1,2,64,256]{3,2,1,0:T(8,128)}) %reduce-scatter.3.cloned.1.call-update) | async-done | bytes 131088 | tf_op jit(solution)/shard_map/reduce_scatter | solution.py:164
  103.0 3.4 %fusion.61 = (f32[1,5,64,256]{3,2,1,0:T(8,128)S(1)}, f32[1,5,64,256]{3,2,1,0:T(8,128)S(1)}) fusion(f32[6,65,257]{2,1,0:T(8,128)} %get-tuple-element.31, f32[6,65,257]{2,1,0:T(8,128)} %broadcast_multiply_fusion.3, f32[6,65,257]{2,1,0:T(8,128)} %get-tuple-element.9, f32[6,65,257]{2,1,0:T(8,128)} %get-tuple-element.30, f32[6,65,257]{2,1,0:T(8,128)S(1)} %copy-done.7, ...), kind=kLoop, calls=%fused_computation.111 | loop fusion | flops 819200 | bytes 4587520 | tf_op jit(solution)/shard_map/stack | solution.py:61
  106.4 31.4 %all-reduce.2.cloned.1.call-done = f32[2,64,256]{2,1,0:T(8,128)} async-done(((f32[2,64,256]{2,1,0:T(8,128)}), f32[2,64,256]{2,1,0:T(8,128)}) %all-reduce.2.cloned.1.call-update) | async-done | bytes 131088 | tf_op jit(solution)/shard_map/psum | solution.py:166
  139.2 3.1 %collective-permute-start.6 = (f32[3,5,64,1]{3,2,1,0:T(8,128)S(1)}, f32[3,5,64,1]{3,2,1,0:T(8,128)S(1)}, u32[]{:S(2)}, u32[]{:S(2)}) collective-permute-start(f32[3,5,64,1]{3,2,1,0:T(8,128)S(1)} %get-tuple-element.24), channel_id=1, source_target_pairs={{0,8},{8,16},{16,24},{1,9},{9,17},{17,25},{2,10},{10,18},{18,26},{... | collective-permute-start | bytes 11528 | tf_op jit(solution)/shard_map/ppermute | solution.py:22
  142.3 2.2 %collective-permute-start.7 = (f32[3,5,64,1]{3,2,1,0:T(8,128)S(1)}, f32[3,5,64,1]{3,2,1,0:T(8,128)S(1)}, u32[]{:S(2)}, u32[]{:S(2)}) collective-permute-start(f32[3,5,64,1]{3,2,1,0:T(8,128)S(1)} %get-tuple-element.25), channel_id=1, source_target_pairs={{8,0},{16,8},{24,16},{9,1},{17,9},{25,17},{10,2},{18,10},{26,18},{... | collective-permute-start | bytes 11528 | tf_op jit(solution)/shard_map/ppermute | solution.py:25
  144.5 7.6 %collective-permute-done.6 = f32[3,5,64,1]{3,2,1,0:T(8,128)S(1)} collective-permute-done((f32[3,5,64,1]{3,2,1,0:T(8,128)S(1)}, f32[3,5,64,1]{3,2,1,0:T(8,128)S(1)}, u32[]{:S(2)}, u32[]{:S(2)}) %collective-permute-start.6) | collective-permute-done | bytes 3872 | tf_op jit(solution)/shard_map/ppermute | solution.py:22
  152.1 2.8 %collective-permute-done.7 = f32[3,5,64,1]{3,2,1,0:T(8,128)S(1)} collective-permute-done((f32[3,5,64,1]{3,2,1,0:T(8,128)S(1)}, f32[3,5,64,1]{3,2,1,0:T(8,128)S(1)}, u32[]{:S(2)}, u32[]{:S(2)}) %collective-permute-start.7) | collective-permute-done | bytes 3872 | tf_op jit(solution)/shard_map/ppermute | solution.py:25
  157.4 4.0 %collective-permute-start.9 = (f32[3,5,1,258]{3,2,1,0:T(1,128)}, f32[3,5,1,258]{3,2,1,0:T(1,128)S(1)}, u32[]{:S(2)}, u32[]{:S(2)}) collective-permute-start(f32[3,5,1,258]{3,2,1,0:T(1,128)} %get-tuple-element.21), channel_id=1, source_target_pairs={{4,0},{5,1},{6,2},{7,3},{12,8},{13,9},{14,10},{15,11},{20,16},{21,... | collective-permute-start | bytes 46448 | tf_op jit(solution)/shard_map/ppermute | solution.py:25
  163.3 6.3 %collective-permute-start.10 = (f32[3,1,66,258]{3,2,1,0:T(8,128)S(1)}, f32[3,1,66,258]{3,2,1,0:T(8,128)S(1)}, u32[]{:S(2)}, u32[]{:S(2)}) collective-permute-start(f32[3,1,66,258]{3,2,1,0:T(8,128)S(1)} %get-tuple-element.16), channel_id=1, source_target_pairs={{0,1},{1,2},{2,3},{4,5},{5,6},{6,7},{8,9},{9,10},{10,11},{12,13},{... | collective-permute-start | bytes 613016 | tf_op jit(solution)/shard_map/ppermute | solution.py:22
  169.7 2.1 %collective-permute-start.11 = (f32[3,1,66,258]{3,2,1,0:T(8,128)S(1)}, f32[3,1,66,258]{3,2,1,0:T(8,128)S(1)}, u32[]{:S(2)}, u32[]{:S(2)}) collective-permute-start(f32[3,1,66,258]{3,2,1,0:T(8,128)S(1)} %get-tuple-element.17), channel_id=1, source_target_pairs={{1,0},{2,1},{3,2},{5,4},{6,5},{7,6},{9,8},{10,9},{11,10},{13,12},{... | collective-permute-start | bytes 613016 | tf_op jit(solution)/shard_map/ppermute | solution.py:25
  171.8 1.9 collective-permute-done.10
  173.7 4.4 %collective-permute-done.11 = f32[3,1,66,258]{3,2,1,0:T(8,128)S(1)} collective-permute-done((f32[3,1,66,258]{3,2,1,0:T(8,128)S(1)}, f32[3,1,66,258]{3,2,1,0:T(8,128)S(1)}, u32[]{:S(2)}, u32[]{:S(2)}) %collective-permute-start.11) | collective-permute-done | bytes 204368 | tf_op jit(solution)/shard_map/ppermute | solution.py:25
  178.1 1.4 fusion.11
  184.0 18.7 %reduce-scatter.5.cloned.1.call-done = f32[2,16,256]{2,1,0:T(8,128)} async-done(((f32[2,64,256]{2,1,0:T(8,128)}), f32[2,16,256]{2,1,0:T(8,128)}) %reduce-scatter.5.cloned.1.call-update) | async-done | bytes 32784 | tf_op jit(solution)/shard_map/reduce_scatter | solution.py:201
  (82 shorter events, 17.9 us)
Async XLA Ops:
  7.2 7.5 %copy-start.16 = (f32[16384]{0:T(1024)S(1)}, f32[16384]{0:T(1024)}, u32[]{:S(2)}) copy-start(f32[16384]{0:T(1024)} %param.17) | copy-start | bytes 196612
  7.2 95.7 %reduce-scatter.3.cloned.1.call-start = ((), (), s32[]{:S(2)}) async-start(), calls=%async_computation.2 | async-start | bytes 1179648 | tf_op jit(solution)/shard_map/reduce_scatter | solution.py:164
  8.6 31.4 %copy-start = (f32[5,64,256]{2,1,0:T(8,128)S(1)}, f32[5,64,256]{2,1,0:T(8,128)}, u32[]{:S(2)}) copy-start(f32[5,64,256]{2,1,0:T(8,128)} %param.12) | copy-start | bytes 983044
  8.6 31.4 %copy-start.1 = (f32[2,5,64,256]{3,2,1,0:T(8,128)S(1)}, f32[2,5,64,256]{3,2,1,0:T(8,128)}, u32[]{:S(2)}) copy-start(f32[2,5,64,256]{3,2,1,0:T(8,128)} %param.11) | copy-start | bytes 1966084
  8.6 31.3 %collective-permute-start = (f32[3,5,64,1]{3,2,1,0:T(8,128)S(1)}, f32[3,5,64,1]{3,2,1,0:T(8,128)S(1)}, u32[]{:S(2)}, u32[]{:S(2)}) collective-permute-start(f32[3,5,64,1]{3,2,1,0:T(8,128)S(1)} %get-tuple-element.26), channel_id=1, source_target_pairs={{0,8},{8,16},{16,24},{1,9},{9,17},{17,25},{2,10},{10,18},{18,26},{... | collective-permute-start | bytes 11528 | tf_op jit(solution)/shard_map/ppermute | solution.py:22
  12.0 28.0 %collective-permute-start.1 = (f32[3,5,64,1]{3,2,1,0:T(8,128)S(1)}, f32[3,5,64,1]{3,2,1,0:T(8,128)S(1)}, u32[]{:S(2)}, u32[]{:S(2)}) collective-permute-start(f32[3,5,64,1]{3,2,1,0:T(8,128)S(1)} %get-tuple-element.27), channel_id=1, source_target_pairs={{8,0},{16,8},{24,16},{9,1},{17,9},{25,17},{10,2},{18,10},{26,18},{... | collective-permute-start | bytes 11528 | tf_op jit(solution)/shard_map/ppermute | solution.py:25
  39.8 98.0 %all-reduce.2.cloned.1.call-start = ((), (), s32[]{:S(2)}) async-start(), calls=%async_computation.3 | async-start | bytes 262144 | tf_op jit(solution)/shard_map/psum | solution.py:166
  40.6 5.3 %collective-permute-start.2 = (f32[3,5,1,258]{3,2,1,0:T(1,128)S(1)}, f32[3,5,1,258]{3,2,1,0:T(1,128)S(1)}, u32[]{:S(2)}, u32[]{:S(2)}) collective-permute-start(f32[3,5,1,258]{3,2,1,0:T(1,128)S(1)} %get-tuple-element.22), channel_id=1, source_target_pairs={{0,4},{1,5},{2,6},{3,7},{8,12},{9,13},{10,14},{11,15},{16,20},{17,... | collective-permute-start | bytes 46448 | tf_op jit(solution)/shard_map/ppermute | solution.py:22
  41.9 4.9 %collective-permute-start.3 = (f32[3,5,1,258]{3,2,1,0:T(1,128)S(1)}, f32[3,5,1,258]{3,2,1,0:T(1,128)S(1)}, u32[]{:S(2)}, u32[]{:S(2)}) collective-permute-start(f32[3,5,1,258]{3,2,1,0:T(1,128)S(1)} %get-tuple-element.23), channel_id=1, source_target_pairs={{4,0},{5,1},{6,2},{7,3},{12,8},{13,9},{14,10},{15,11},{20,16},{21,... | collective-permute-start | bytes 46448 | tf_op jit(solution)/shard_map/ppermute | solution.py:25
  45.9 8.9 %copy-start.9 = (f32[64,256]{1,0:T(8,128)S(1)}, f32[64,256]{1,0:T(8,128)}, u32[]{:S(2)}) copy-start(f32[64,256]{1,0:T(8,128)} %param.13) | copy-start | bytes 196612
  47.5 9.4 %collective-permute-start.4 = (f32[3,1,66,258]{3,2,1,0:T(8,128)S(1)}, f32[3,1,66,258]{3,2,1,0:T(8,128)S(1)}, u32[]{:S(2)}, u32[]{:S(2)}) collective-permute-start(f32[3,1,66,258]{3,2,1,0:T(8,128)S(1)} %get-tuple-element.18), channel_id=1, source_target_pairs={{0,1},{1,2},{2,3},{4,5},{5,6},{6,7},{8,9},{9,10},{10,11},{12,13},{... | collective-permute-start | bytes 613016 | tf_op jit(solution)/shard_map/ppermute | solution.py:22
  52.9 8.8 %collective-permute-start.5 = (f32[3,1,66,258]{3,2,1,0:T(8,128)S(1)}, f32[3,1,66,258]{3,2,1,0:T(8,128)S(1)}, u32[]{:S(2)}, u32[]{:S(2)}) collective-permute-start(f32[3,1,66,258]{3,2,1,0:T(8,128)S(1)} %get-tuple-element.19), channel_id=1, source_target_pairs={{1,0},{2,1},{3,2},{5,4},{6,5},{7,6},{9,8},{10,9},{11,10},{13,12},{... | collective-permute-start | bytes 613016 | tf_op jit(solution)/shard_map/ppermute | solution.py:25
  55.0 83.7 %copy-start.3 = (f32[5,64,256]{2,1,0:T(8,128)}, f32[5,64,256]{2,1,0:T(8,128)S(1)}, u32[]{:S(2)}) copy-start(f32[5,64,256]{2,1,0:T(8,128)S(1)} %get-tuple-element.36) | copy-start | bytes 983044
  55.0 83.7 %copy-start.5 = (f32[5,64,256]{2,1,0:T(8,128)}, f32[5,64,256]{2,1,0:T(8,128)S(1)}, u32[]{:S(2)}) copy-start(f32[5,64,256]{2,1,0:T(8,128)S(1)} %get-tuple-element.37) | copy-start | bytes 983044
  65.5 37.4 %copy-start.7 = (f32[6,65,257]{2,1,0:T(8,128)S(1)}, f32[6,65,257]{2,1,0:T(8,128)}, u32[]{:S(2)}) copy-start(f32[6,65,257]{2,1,0:T(8,128)} %get-tuple-element.4) | copy-start | bytes 1202764
  102.9 99.7 %reduce-scatter.5.cloned.1.call-start = ((), (), s32[]{:S(2)}) async-start(), calls=%async_computation.4 | async-start | bytes 163840 | tf_op jit(solution)/shard_map/reduce_scatter | solution.py:201
  139.2 12.9 %collective-permute-start.6 = (f32[3,5,64,1]{3,2,1,0:T(8,128)S(1)}, f32[3,5,64,1]{3,2,1,0:T(8,128)S(1)}, u32[]{:S(2)}, u32[]{:S(2)}) collective-permute-start(f32[3,5,64,1]{3,2,1,0:T(8,128)S(1)} %get-tuple-element.24), channel_id=1, source_target_pairs={{0,8},{8,16},{16,24},{1,9},{9,17},{17,25},{2,10},{10,18},{18,26},{... | collective-permute-start | bytes 11528 | tf_op jit(solution)/shard_map/ppermute | solution.py:22
  142.3 12.6 %collective-permute-start.7 = (f32[3,5,64,1]{3,2,1,0:T(8,128)S(1)}, f32[3,5,64,1]{3,2,1,0:T(8,128)S(1)}, u32[]{:S(2)}, u32[]{:S(2)}) collective-permute-start(f32[3,5,64,1]{3,2,1,0:T(8,128)S(1)} %get-tuple-element.25), channel_id=1, source_target_pairs={{8,0},{16,8},{24,16},{9,1},{17,9},{25,17},{10,2},{18,10},{26,18},{... | collective-permute-start | bytes 11528 | tf_op jit(solution)/shard_map/ppermute | solution.py:25
  156.2 5.3 %collective-permute-start.8 = (f32[3,5,1,258]{3,2,1,0:T(1,128)}, f32[3,5,1,258]{3,2,1,0:T(1,128)S(1)}, u32[]{:S(2)}, u32[]{:S(2)}) collective-permute-start(f32[3,5,1,258]{3,2,1,0:T(1,128)} %get-tuple-element.20), channel_id=1, source_target_pairs={{0,4},{1,5},{2,6},{3,7},{8,12},{9,13},{10,14},{11,15},{16,20},{17,... | collective-permute-start | bytes 46448 | tf_op jit(solution)/shard_map/ppermute | solution.py:22
  157.4 5.1 %collective-permute-start.9 = (f32[3,5,1,258]{3,2,1,0:T(1,128)}, f32[3,5,1,258]{3,2,1,0:T(1,128)S(1)}, u32[]{:S(2)}, u32[]{:S(2)}) collective-permute-start(f32[3,5,1,258]{3,2,1,0:T(1,128)} %get-tuple-element.21), channel_id=1, source_target_pairs={{4,0},{5,1},{6,2},{7,3},{12,8},{13,9},{14,10},{15,11},{20,16},{21,... | collective-permute-start | bytes 46448 | tf_op jit(solution)/shard_map/ppermute | solution.py:25
  161.4 10.3 %copy-start.11 = (f32[2,64,256]{2,1,0:T(8,128)S(1)}, f32[2,64,256]{2,1,0:T(8,128)}, u32[]{:S(2)}) copy-start(f32[2,64,256]{2,1,0:T(8,128)} %param.15) | copy-start | bytes 393220
  163.3 10.4 %collective-permute-start.10 = (f32[3,1,66,258]{3,2,1,0:T(8,128)S(1)}, f32[3,1,66,258]{3,2,1,0:T(8,128)S(1)}, u32[]{:S(2)}, u32[]{:S(2)}) collective-permute-start(f32[3,1,66,258]{3,2,1,0:T(8,128)S(1)} %get-tuple-element.16), channel_id=1, source_target_pairs={{0,1},{1,2},{2,3},{4,5},{5,6},{6,7},{8,9},{9,10},{10,11},{12,13},{... | collective-permute-start | bytes 613016 | tf_op jit(solution)/shard_map/ppermute | solution.py:22
  169.7 8.4 %collective-permute-start.11 = (f32[3,1,66,258]{3,2,1,0:T(8,128)S(1)}, f32[3,1,66,258]{3,2,1,0:T(8,128)S(1)}, u32[]{:S(2)}, u32[]{:S(2)}) collective-permute-start(f32[3,1,66,258]{3,2,1,0:T(8,128)S(1)} %get-tuple-element.17), channel_id=1, source_target_pairs={{1,0},{2,1},{3,2},{5,4},{6,5},{7,6},{9,8},{10,9},{11,10},{13,12},{... | collective-permute-start | bytes 613016 | tf_op jit(solution)/shard_map/ppermute | solution.py:25
  182.6 20.0 %copy-start.2 = (f32[2,5,64,256]{3,2,1,0:T(8,128)}, f32[2,5,64,256]{3,2,1,0:T(8,128)S(1)}, u32[]{:S(2)}) copy-start(f32[2,5,64,256]{3,2,1,0:T(8,128)S(1)} %fusion.47) | copy-start | bytes 1966084
  (8 other events, 19.8 us)
Sparse Core Ops, SparseCore 0:
  39.9 62.8 reduce-scatter.2
  105.2 32.5 all-reduce.1
  184.1 18.4 reduce-scatter.4

commit v2 on v1

v2 whole, which is shorter than its diff:
```python
import functools

import jax
import jax.numpy as jnp
from jax import lax
from jax.experimental import pallas as pl
from jax.experimental.pallas import tpu as pltpu
from jax.sharding import PartitionSpec as P

ITERS = 2


OMEGA = 0.6
VERTICAL = 4.0


def bin_kernel(tiles, rows, cols, fx_ref, fy_ref, tile_ref, cell_ref, out_ref, lhs, rhs):
    step = pl.program_id(0)
    depth = fx_ref.shape[1]
    tile = tile_ref[...]
    cell = cell_ref[...]
    col = lax.rem(cell, cols).astype(jnp.float32).astype(jnp.bfloat16)
    row = lax.div(cell, cols).astype(jnp.float32)
    fx = fx_ref[...]
    fy = fy_ref[...]
    fx_hi = fx.astype(jnp.bfloat16)
    fy_hi = fy.astype(jnp.bfloat16)
    fx_lo = (fx - fx_hi.astype(jnp.float32)).astype(jnp.bfloat16)
    fy_lo = (fy - fy_hi.astype(jnp.float32)).astype(jnp.bfloat16)
    x_ids = lax.broadcasted_iota(jnp.int32, (cols, depth), 0).astype(jnp.float32).astype(jnp.bfloat16)
    one = jnp.ones((cols, depth), jnp.bfloat16)
    rhs[...] = jnp.where(x_ids == col, one, jnp.zeros_like(one))
    y_ids = lax.broadcasted_iota(jnp.int32, (rows, depth), 0).astype(jnp.float32).astype(jnp.bfloat16)
    zero = jnp.zeros((rows, depth), jnp.bfloat16)
    for t in range(tiles):
        own = jnp.where(tile == t, row, -1.0).astype(jnp.bfloat16)
        hit = y_ids == own
        for c, piece in enumerate((fx_hi, fy_hi, fx_lo, fy_lo)):
            part = c // 2
            start = (t * 2 + c % 2) * rows
            lhs[part, start : start + rows, :] = jnp.where(hit, jnp.broadcast_to(piece, (rows, depth)), zero)
    total = lax.dot_general(
        lhs[0], rhs[...], (((1,), (1,)), ((), ())), preferred_element_type=jnp.float32
    ) + lax.dot_general(
        lhs[1], rhs[...], (((1,), (1,)), ((), ())), preferred_element_type=jnp.float32
    )

    @pl.when(step == 0)
    def _():
        out_ref[...] = total

    @pl.when(step > 0)
    def _():
        out_ref[...] += total


def bin_pixels(fx, fy, tile, cell, tiles, rows, cols):
    per_device = fx.shape[0]
    depth = min(1024, per_device)
    while depth * tiles * rows * 8 > 24 * 2**20:
        depth //= 2
    steps = per_device // depth
    flat = [value.reshape(steps, 1, depth) for value in (fx, fy, tile, cell)]
    spec = pl.BlockSpec((None, 1, depth), lambda i: (i, 0, 0))
    sums = pl.pallas_call(
        functools.partial(bin_kernel, tiles, rows, cols),
        grid=(steps,),
        in_specs=[spec] * 4,
        out_specs=pl.BlockSpec((tiles * 2 * rows, cols), lambda i: (0, 0)),
        out_shape=jax.ShapeDtypeStruct((tiles * 2 * rows, cols), jnp.float32),
        scratch_shapes=[
            pltpu.VMEM((2, tiles * 2 * rows, depth), jnp.bfloat16),
            pltpu.VMEM((cols, depth), jnp.bfloat16),
        ],
        name="bin_pixels",
    )(*flat)
    return sums.reshape(tiles, 2, rows, cols)


def lane_column(pack, lane, like):
    return jnp.broadcast_to(pack[:, lane : lane + 1], like.shape)


def from_east(value, column):
    size = value.shape[1]
    lanes = lax.broadcasted_iota(jnp.int32, value.shape, 1)
    return jnp.where(lanes == size - 1, column, pltpu.roll(value, size - 1, 1))


def from_west(value, column):
    lanes = lax.broadcasted_iota(jnp.int32, value.shape, 1)
    return jnp.where(lanes == 0, column, pltpu.roll(value, 1, 1))


def from_north(value, row):
    size = value.shape[0]
    rows = lax.broadcasted_iota(jnp.int32, value.shape, 0)
    return jnp.where(rows == size - 1, row, pltpu.roll(value, size - 1, 0))


def from_south(value, row):
    rows = lax.broadcasted_iota(jnp.int32, value.shape, 0)
    return jnp.where(rows == 0, row, pltpu.roll(value, 1, 0))


def apply_kernel(
    counts,
    sums,
    guess,
    visc,
    fric,
    base,
    slope,
    mask,
    adj_out,
    maps_out,
    *scratch,
):
    nx, ny, nz = counts
    bits = nz.bit_length() - 1
    tiles = nx * ny
    layers, rows, cols = visc.shape
    scratch = list(scratch)
    accs = [scratch.pop(0) for _ in range(bits)]
    recvs = [scratch.pop(0) for _ in range(bits)]
    (
        tile_in,
        block,
        forcing,
        middle,
        west_edge,
        east_edge,
        south_edge,
        north_edge,
        halo_w,
        halo_e,
        halo_s,
        halo_n,
        halo_se,
        halo_nw,
        halo_d,
        halo_u,
        visc_d,
        part,
        part_in,
        half_sem,
        tile_sem,
        last_send,
        last_recv,
        halo_sem,
        visc_sem,
        part_sem,
    ) = scratch
    gx, gy, gz = lax.axis_index("gx"), lax.axis_index("gy"), lax.axis_index("gz")
    tile = gx * ny + gy
    lane_step = 16
    row_step = 8

    def remote(src, dst, send, recv, device):
        return pltpu.make_async_remote_copy(
            src_ref=src,
            dst_ref=dst,
            send_sem=send,
            recv_sem=recv,
            device_id=device,
            device_id_type=pl.DeviceIdType.MESH,
        )

    barrier = pltpu.get_barrier_semaphore()
    layer_peers = [(gx, gy, lax.rem(gz + o, nz)) for o in range(1, nz)]
    tile_peers = []
    for o in range(1, tiles):
        other = lax.rem(tile + o, tiles)
        tile_peers.append((other, (lax.div(other, ny), lax.rem(other, ny), gz)))
    for device in layer_peers + [device for _, device in tile_peers]:
        pl.semaphore_signal(barrier, inc=1, device_id=device, device_id_type=pl.DeviceIdType.MESH)
    pl.semaphore_wait(barrier, nz - 1 + tiles - 1)

    size = rows // 2
    starts = []
    offset = jnp.int32(0)
    for bit in range(bits):
        own_bit = lax.rem(lax.div(gz, 1 << bit), 2)
        keep = pl.multiple_of(own_bit * size, size)
        give = pl.multiple_of((1 - own_bit) * size, size)
        peer = (gx, gy, gz + (1 - 2 * own_bit) * (1 << bit))
        starts.append((keep, give, size, peer))
        offset = offset + own_bit * size
        size //= 2
    size = rows // nz
    offset = pl.multiple_of(offset, size)

    def half_copy(bit):
        _, give, length, peer = starts[bit]
        source = sums if bit == 0 else accs[bit - 1]
        return remote(
            source.at[:, :, pl.ds(give, length), :],
            recvs[bit],
            half_sem.at[0, bit],
            half_sem.at[1, bit],
            peer,
        )

    half_copy(0).start()

    def pack(field):
        lanes = lax.broadcasted_iota(jnp.int32, (rows, 128), 1)
        west = jnp.zeros((rows, 128), jnp.float32)
        east = jnp.zeros((rows, 128), jnp.float32)
        for f in range(3):
            for k in range(layers):
                value = field[f, k] if f < 2 else visc[k]
                south_edge[f * row_step + k : f * row_step + k + 1, :] = value[0:1, :]
                north_edge[f * row_step + k : f * row_step + k + 1, :] = value[rows - 1 : rows, :]
                lane = lanes == f * lane_step + k
                west = jnp.where(lane, lane_column(value, 0, west), west)
                east = jnp.where(lane, lane_column(value, cols - 1, east), east)
        west_edge[...] = west
        east_edge[...] = east

    def halo_copies(field, turn):
        def one(index, src, dst, device):
            return remote(src, dst, halo_sem.at[turn, 0, index], halo_sem.at[turn, 1, index], device)

        return [
            (one(0, west_edge, halo_e.at[turn], (gx - 1, gy, gz)), gx > 0, gx < nx - 1),
            (one(1, east_edge, halo_w.at[turn], (gx + 1, gy, gz)), gx < nx - 1, gx > 0),
            (one(2, south_edge, halo_n.at[turn], (gx, gy - 1, gz)), gy > 0, gy < ny - 1),
            (one(3, north_edge, halo_s.at[turn], (gx, gy + 1, gz)), gy < ny - 1, gy > 0),
            (
                one(4, north_edge.at[:, 0:128], halo_se.at[turn], (gx - 1, gy + 1, gz)),
                (gx > 0) & (gy < ny - 1),
                (gx < nx - 1) & (gy > 0),
            ),
            (
                one(5, east_edge.at[0:8, :], halo_nw.at[turn], (gx + 1, gy - 1, gz)),
                (gx < nx - 1) & (gy > 0),
                (gx > 0) & (gy < ny - 1),
            ),
            (one(6, field.at[:, 0], halo_u.at[turn], (gx, gy, gz - 1)), gz > 0, gz < nz - 1),
            (one(7, field.at[:, layers - 1], halo_d.at[turn], (gx, gy, gz + 1)), gz < nz - 1, gz > 0),
        ]

    def start_all(copies):
        for copy, sends, _ in copies:

            @pl.when(sends)
            def _(copy=copy):
                copy.start()

    def wait_all(copies):
        for copy, sends, receives in copies:

            @pl.when(receives)
            def _(copy=copy):
                copy.wait_recv()

            @pl.when(sends)
            def _(copy=copy):
                copy.wait_send()

    pack(guess)
    visc_up = (
        remote(visc.at[layers - 1], visc_d, visc_sem.at[0], visc_sem.at[1], (gx, gy, gz + 1)),
        gz < nz - 1,
        gz > 0,
    )
    first = halo_copies(guess, 0) + [visc_up]
    start_all(first)

    mask_float = mask[...].astype(jnp.float32)
    lane_ids = lax.broadcasted_iota(jnp.int32, (rows, cols), 1)
    row_ids = lax.broadcasted_iota(jnp.int32, (rows, cols), 0)
    mx = jnp.where((lane_ids < cols - 1) | (gx < nx - 1), 1.0, 0.0)
    my = jnp.where((row_ids < rows - 1) | (gy < ny - 1), 1.0, 0.0)
    my_col = my[:, 0:128]
    mx_row = mx[0:8, :]
    west_on = jnp.where(gx > 0, 1.0, 0.0)
    up_on = jnp.where(gz < nz - 1, 1.0, 0.0)

    def damping_of(k):
        scale = 18.0 * visc[k]
        if k == 0:
            scale = scale + jnp.where(gz == 0, fric[...], 0.0)
        return 0.6 / scale

    def sweep(field, turn, store):
        west = jnp.where(gx > 0, halo_w[turn], 0.0)
        east = jnp.where(gx < nx - 1, halo_e[turn], 0.0)
        south = jnp.where(gy > 0, halo_s[turn], 0.0)
        north = jnp.where(gy < ny - 1, halo_n[turn], 0.0)
        corner_se = jnp.where((gx < nx - 1) & (gy > 0), halo_se[turn], 0.0)
        corner_nw = jnp.where((gx > 0) & (gy < ny - 1), halo_nw[turn], 0.0)
        own_w = west_edge[...]
        own_s = south_edge[...]

        west_b = pltpu.roll(west, 128 - lane_step, 1)
        west_v = pltpu.roll(west, 128 - 2 * lane_step, 1)
        corner_b = pltpu.roll(corner_nw, 128 - lane_step, 1)
        col_na = (from_north(west, corner_nw[0:1, :]) - west) * my_col
        col_nb = (from_north(west_b, corner_b[0:1, :]) - west_b) * my_col
        col_ea = (own_w - west) * west_on
        col_eb = (pltpu.roll(own_w, 128 - lane_step, 1) - west_b) * west_on
        col_p = west_v * (4.0 * col_ea + 2.0 * col_nb) * west_on
        col_s = west_v * (col_na + col_eb) * west_on

        south_a, south_b, south_v = south[0:8], south[8:16], south[16:24]
        south_on = jnp.where(gy > 0, 1.0, 0.0)
        row_ea = (from_east(south_a, lane_column(corner_se[0:8], 0, south_a)) - south_a) * mx_row
        row_eb = (from_east(south_b, lane_column(corner_se[8:16], 0, south_b)) - south_b) * mx_row
        row_na = (own_s[0:8] - south_a) * south_on
        row_nb = (own_s[8:16] - south_b) * south_on
        row_q = south_v * (4.0 * row_nb + 2.0 * row_ea) * south_on
        row_s = south_v * (row_na + row_eb) * south_on

        below_v = jnp.where(gz > 0, visc_d[...], 0.0)
        low_a = 4.0 * below_v * (field[0, 0] - jnp.where(gz > 0, halo_d[turn, 0], 0.0))
        low_b = 4.0 * below_v * (field[1, 0] - jnp.where(gz > 0, halo_d[turn, 1], 0.0))
        for k in range(layers):
            va, vb, v = field[0, k], field[1, k], visc[k]
            ea = (from_east(va, lane_column(east, k, va)) - va) * mx
            eb = (from_east(vb, lane_column(east, lane_step + k, vb)) - vb) * mx
            na = (from_north(va, north[k : k + 1]) - va) * my
            nb = (from_north(vb, north[row_step + k : row_step + k + 1]) - vb) * my
            p = mx * v * (4.0 * ea + 2.0 * nb)
            q = my * v * (4.0 * nb + 2.0 * ea)
            s = v * (na + eb)
            sx = mx * s
            sy = my * s
            if k < layers - 1:
                top_a = 4.0 * v * (field[0, k + 1] - va)
                top_b = 4.0 * v * (field[1, k + 1] - vb)
            else:
                top_a = 4.0 * v * (jnp.where(gz < nz - 1, halo_u[turn, 0], 0.0) - va) * up_on
                top_b = 4.0 * v * (jnp.where(gz < nz - 1, halo_u[turn, 1], 0.0) - vb) * up_on
            image_a = (
                (from_west(p, lane_column(col_p, k, p)) - p)
                + (from_south(sy, row_s[k : k + 1]) - sy)
                + (low_a - top_a)
            )
            image_b = (
                (from_south(q, row_q[k : k + 1]) - q)
                + (from_west(sx, lane_column(col_s, k, sx)) - sx)
                + (low_b - top_b)
            )
            if k == 0:
                basal = jnp.where(gz == 0, fric[...], 0.0)
                image_a = image_a + basal * va
                image_b = image_b + basal * vb
            low_a, low_b = top_a, top_b
            damp = damping_of(k)
            store(k, va, vb, damp, image_a, image_b)

    def store_first(k, va, vb, damp, image_a, image_b):
        middle[0, k] = va - damp * image_a
        middle[1, k] = vb - damp * image_b

    for bit in range(bits):
        keep, give, length, _ = starts[bit]
        source = sums if bit == 0 else accs[bit - 1]
        copy = half_copy(bit)
        copy.wait_recv()
        if bit + 1 < bits:
            next_keep, next_give, next_length, _ = starts[bit + 1]
            for begin in (next_give, next_keep):
                accs[bit][:, :, pl.ds(begin, next_length), :] = (
                    source[:, :, pl.ds(pl.multiple_of(keep + begin, next_length), next_length), :]
                    + recvs[bit][:, :, pl.ds(begin, next_length), :]
                )
                if begin is next_give:
                    half_copy(bit + 1).start()
        else:
            accs[bit][...] = source[:, :, pl.ds(keep, length), :] + recvs[bit][...]
        if bit == bits - 2 or bits == 1:
            wait_all(first)
            sweep(guess, 0, store_first)
    total = accs[bits - 1]

    def tile_copy(o):
        other, device = tile_peers[o - 1]
        return remote(total.at[other], tile_in.at[o - 1], tile_sem.at[0, o - 1], tile_sem.at[1, o - 1], device)

    for o in range(1, tiles):
        tile_copy(o).start()
    value = total[tile]
    for o in range(1, tiles):
        tile_copy(o).wait_recv()
        value = value + tile_in[o - 1]
    block[...] = value

    def row_start(j):
        begin = 0
        length = rows // 2
        for bit in range(bits):
            begin += ((j >> bit) & 1) * length
            length //= 2
        return begin

    to_last = remote(
        block, forcing.at[:, pl.ds(offset, size), :], last_send, last_recv.at[gz], (gx, gy, nz - 1)
    )

    @pl.when(gz < nz - 1)
    def _():
        to_last.start()

    @pl.when(gz == nz - 1)
    def _():
        begin = row_start(nz - 1)
        forcing[:, begin : begin + size, :] = block[...]
        for j in range(nz - 1):
            begin = row_start(j)
            remote(
                block,
                forcing.at[:, begin : begin + size, :],
                last_send,
                last_recv.at[j],
                (gx, gy, 0),
            ).wait_recv()
        damp = damping_of(layers - 1)
        middle[0, layers - 1] = middle[0, layers - 1] + damp * (forcing[0] * mask_float)
        middle[1, layers - 1] = middle[1, layers - 1] + damp * (forcing[1] * mask_float)

    pack(middle)
    second = halo_copies(middle, 1)
    start_all(second)
    wait_all(second)

    on_base = jnp.where(gz == 0, 1.0, 0.0)
    drive = []

    def store_second(k, va, vb, damp, image_a, image_b):
        new_a = va - damp * image_a
        new_b = vb - damp * image_b
        if k == layers - 1:
            rhs_a = jnp.where(gz == nz - 1, forcing[0] * mask_float, 0.0)
            rhs_b = jnp.where(gz == nz - 1, forcing[1] * mask_float, 0.0)
            new_a = va + damp * (rhs_a - image_a)
            new_b = vb + damp * (rhs_b - image_b)
        adj_out[0, k] = new_a
        adj_out[1, k] = new_b
        term = slope[0] * new_a + slope[1] * new_b
        if k == 0:
            part[0] = -on_base * mask_float * fric[...] * (base[0] * new_a + base[1] * new_b)
            part[1] = term
        else:
            part[1] = part[1] + term

    sweep(middle, 1, store_second)
    part[1] = 0.25 * mask_float * part[1]

    def part_copy(o):
        device = layer_peers[o - 1]
        begin = pl.multiple_of(device[2] * size, size)
        return remote(
            part.at[:, pl.ds(begin, size), :],
            part_in.at[o - 1],
            part_sem.at[0, o - 1],
            part_sem.at[1, o - 1],
            device,
        )

    for o in range(1, nz):
        part_copy(o).start()
    value = part[:, pl.ds(pl.multiple_of(gz * size, size), size), :]
    for o in range(1, nz):
        part_copy(o).wait_recv()
        value = value + part_in[o - 1]
    maps_out[...] = value

    for bit in range(bits):
        half_copy(bit).wait_send()
    for o in range(1, tiles):
        tile_copy(o).wait_send()

    @pl.when(gz < nz - 1)
    def _():
        to_last.wait_send()

    for o in range(1, nz):
        part_copy(o).wait_send()


def apply_twice(sums, guess, visc, fric, base, slope, mask, counts):
    nx, ny, nz = counts
    tiles = nx * ny
    bits = nz.bit_length() - 1
    _, layers, rows, cols = guess.shape
    size = rows // nz
    f32 = jnp.float32
    halves = [pltpu.VMEM((tiles, 2, rows >> (bit + 1), cols), f32) for bit in range(bits)]
    vmem = pl.BlockSpec(memory_space=pltpu.VMEM)
    dma = pltpu.SemaphoreType.DMA
    return pl.pallas_call(
        functools.partial(apply_kernel, counts),
        in_specs=[vmem] * 7,
        out_specs=(vmem, vmem),
        out_shape=(
            jax.ShapeDtypeStruct(guess.shape, f32),
            jax.ShapeDtypeStruct((2, size, cols), f32),
        ),
        scratch_shapes=halves
        + halves
        + [
            pltpu.VMEM((tiles - 1, 2, size, cols), f32),
            pltpu.VMEM((2, size, cols), f32),
            pltpu.VMEM((2, rows, cols), f32),
            pltpu.VMEM(guess.shape, f32),
            pltpu.VMEM((rows, 128), f32),
            pltpu.VMEM((rows, 128), f32),
            pltpu.VMEM((24, cols), f32),
            pltpu.VMEM((24, cols), f32),
            pltpu.VMEM((2, rows, 128), f32),
            pltpu.VMEM((2, rows, 128), f32),
            pltpu.VMEM((2, 24, cols), f32),
            pltpu.VMEM((2, 24, cols), f32),
            pltpu.VMEM((2, 24, 128), f32),
            pltpu.VMEM((2, 8, 128), f32),
            pltpu.VMEM((2, 2, rows, cols), f32),
            pltpu.VMEM((2, 2, rows, cols), f32),
            pltpu.VMEM((rows, cols), f32),
            pltpu.VMEM((2, rows, cols), f32),
            pltpu.VMEM((nz - 1, 2, size, cols), f32),
            dma((2, bits)),
            dma((2, tiles - 1)),
            dma,
            dma((nz,)),
            dma((2, 2, 8)),
            dma((2,)),
            dma((2, nz - 1)),
        ],
        compiler_params=pltpu.CompilerParams(
            collective_id=0, has_side_effects=True, vmem_limit_bytes=56 * 2**20
        ),
        name="apply_twice",
    )(sums, guess, visc, fric, base, slope, mask)


def body(
    adjoint_guess,
    viscosity,
    friction,
    base_velocity,
    surface_slope,
    ice_mask,
    pixel_misfit,
    pixel_look,
    pixel_tile,
    pixel_cell,
    pixel_count,
):
    rows_local = adjoint_guess.shape[2]
    cols_local = adjoint_guess.shape[3]
    count_x = lax.axis_size("gx")
    count_y = lax.axis_size("gy")
    count_z = lax.axis_size("gz")
    tile_total = count_x * count_y
    per_device = pixel_misfit.shape[0]
    live = jnp.arange(per_device, dtype=jnp.int32) < pixel_count[0]
    values = jnp.where(live, pixel_misfit, jnp.float32(0.0))
    sums = bin_pixels(
        values * jnp.cos(pixel_look),
        values * jnp.sin(pixel_look),
        pixel_tile[:, 0],
        pixel_cell,
        tile_total,
        rows_local,
        cols_local,
    )
    return apply_twice(
        sums,
        adjoint_guess,
        viscosity,
        friction,
        base_velocity,
        surface_slope,
        ice_mask,
        (count_x, count_y, count_z),
    )


def solution(mesh):
    return jax.shard_map(
        body,
        mesh=mesh,
        in_specs=(
            P(None, "gz", "gy", "gx"),
            P("gz", "gy", "gx"),
            P("gy", "gx"),
            P(None, "gy", "gx"),
            P(None, "gy", "gx"),
            P("gy", "gx"),
            P(("gx", "gy", "gz")),
            P(("gx", "gy", "gz")),
            P(("gx", "gy", "gz"), None),
            P(("gx", "gy", "gz")),
            P(("gx", "gy", "gz")),
        ),
        out_specs=(P(None, "gz", "gy", "gx"), P(None, ("gy", "gz"), "gx")),
        check_vma=False,
    )
```

time: 212 us -> 64.2 us (0.30)
  the two profiles are of different devices: /device:TPU:21 before, /device:TPU:0 now
where the time goes in v2:
time: 64.2 us; the launch traced here: 64 us
  Pallas kernels  58.3 us (91%)
  local copies, waits for them, and re-layouts  2.6 us (4%)
  other arithmetic  1.77 us (3%)
  between operations  1.29 us (2%)
    pallas_call x1, Pallas kernels, apply_twice(): pl.pallas_call(functools.partial(apply_kernel, counts), in_specs=[vmem] *...  34.2 us
    pallas_call x1, Pallas kernels, bin_pixels(): pl.pallas_call(functools.partial(bin_kernel, tiles, rows, cols), grid=(st...  24.1 us
    unnamed x4, local copies, waits for them, and re-layouts  2.6 us
    mul x1, other arithmetic, body(): values * jnp.sin(pixel_look)  1.77 us

profile of v2, /device:TPU:0, one launch (start us, length us, event | category | flops | bytes accessed | tf_op | source)
XLA Modules:
  0.0 64.0 jit_solution(2927480016234698858)
XLA Ops:
  1.3 1.8 %sine_multiply_fusion = (f32[16384]{0:T(1024)}, f32[16384]{0:T(1024)}) fusion(f32[16384]{0:T(1024)} %param.18, f32[16384]{0:T(1024)} %param.17, s32[]{:T(128)} %bitcast.6), kind=kLoop, calls=%fused_computation | loop fusion | flops 65536 | bytes 262148 | tf_op jit(solution)/shard_map/mul | solution.py:563
  3.0 24.1 %bin_pixels.1 = f32[1024,256]{1,0:T(8,128)} custom-call(f32[16,1,1024]{2,1,0:T(1,128)} %bitcast.9, f32[16,1,1024]{2,1,0:T(1,128)} %bitcast.8, s32[16,1,1024]{2,1,0:T(1,128)} %bitcast.10, s32[16,1,1024]{2,1,0:T(1,128)} %bitcast.11), custom_call_target="tpu_custom_call" | custom-call | tf_op jit(solution)/shard_map/bin_pixels/pallas_call | solution.py:65
  27.2 34.2 %apply_twice.1 = (f32[2,5,64,256]{3,2,1,0:T(8,128)}, f32[2,16,256]{2,1,0:T(8,128)}) custom-call(f32[8,2,64,256]{3,2,1,0:T(8,128)} %bitcast.7, f32[2,5,64,256]{3,2,1,0:T(8,128)} %guess.1, f32[5,64,256]{2,1,0:T(8,128)} %visc.1, f32[64,256]{1,0:T(8,128)} %fric.1, f32[2,64,256]{2,1,0:T(8,128)} %base.1, f32[2,64,256]{2,1,0:T(8,128)} %slope.1, s32[64,256]{1,0:T(8,128)} %mask.1), custom_call_target="tpu_custom_call" | custom-call | tf_op jit(solution)/shard_map/apply_twice/pallas_call | solution.py:494
  61.4 0.0 copy-start
  61.4 2.0 %copy.16 = f32[2,5,64,256]{3,2,1,0:T(8,128)} copy(f32[2,5,64,256]{3,2,1,0:T(8,128)} %get-tuple-element.6) | data formatting | bytes 1310720
  63.4 0.0 copy-done
  63.4 0.6 copy.17
Async XLA Ops:
  61.4 2.0 %copy-start = (f32[2,16,256]{2,1,0:T(8,128)S(1)}, f32[2,16,256]{2,1,0:T(8,128)}, u32[]{:S(2)}) copy-start(f32[2,16,256]{2,1,0:T(8,128)} %get-tuple-element.7) | copy-start | bytes 98308

commit v3 on v2

--- a/solution.py
+++ b/solution.py
@@ -7,74 +7,8 @@
 from jax.experimental.pallas import tpu as pltpu
 from jax.sharding import PartitionSpec as P
 
-ITERS = 2
-
-
-OMEGA = 0.6
-VERTICAL = 4.0
-
-
-def bin_kernel(tiles, rows, cols, fx_ref, fy_ref, tile_ref, cell_ref, out_ref, lhs, rhs):
-    step = pl.program_id(0)
-    depth = fx_ref.shape[1]
-    tile = tile_ref[...]
-    cell = cell_ref[...]
-    col = lax.rem(cell, cols).astype(jnp.float32).astype(jnp.bfloat16)
-    row = lax.div(cell, cols).astype(jnp.float32)
-    fx = fx_ref[...]
-    fy = fy_ref[...]
-    fx_hi = fx.astype(jnp.bfloat16)
-    fy_hi = fy.astype(jnp.bfloat16)
-    fx_lo = (fx - fx_hi.astype(jnp.float32)).astype(jnp.bfloat16)
-    fy_lo = (fy - fy_hi.astype(jnp.float32)).astype(jnp.bfloat16)
-    x_ids = lax.broadcasted_iota(jnp.int32, (cols, depth), 0).astype(jnp.float32).astype(jnp.bfloat16)
-    one = jnp.ones((cols, depth), jnp.bfloat16)
-    rhs[...] = jnp.where(x_ids == col, one, jnp.zeros_like(one))
-    y_ids = lax.broadcasted_iota(jnp.int32, (rows, depth), 0).astype(jnp.float32).astype(jnp.bfloat16)
-    zero = jnp.zeros((rows, depth), jnp.bfloat16)
-    for t in range(tiles):
-        own = jnp.where(tile == t, row, -1.0).astype(jnp.bfloat16)
-        hit = y_ids == own
-        for c, piece in enumerate((fx_hi, fy_hi, fx_lo, fy_lo)):
-            part = c // 2
-            start = (t * 2 + c % 2) * rows
-            lhs[part, start : start + rows, :] = jnp.where(hit, jnp.broadcast_to(piece, (rows, depth)), zero)
-    total = lax.dot_general(
-        lhs[0], rhs[...], (((1,), (1,)), ((), ())), preferred_element_type=jnp.float32
-    ) + lax.dot_general(
-        lhs[1], rhs[...], (((1,), (1,)), ((), ())), preferred_element_type=jnp.float32
-    )
-
-    @pl.when(step == 0)
-    def _():
-        out_ref[...] = total
-
-    @pl.when(step > 0)
-    def _():
-        out_ref[...] += total
-
-
-def bin_pixels(fx, fy, tile, cell, tiles, rows, cols):
-    per_device = fx.shape[0]
-    depth = min(1024, per_device)
-    while depth * tiles * rows * 8 > 24 * 2**20:
-        depth //= 2
-    steps = per_device // depth
-    flat = [value.reshape(steps, 1, depth) for value in (fx, fy, tile, cell)]
-    spec = pl.BlockSpec((None, 1, depth), lambda i: (i, 0, 0))
-    sums = pl.pallas_call(
-        functools.partial(bin_kernel, tiles, rows, cols),
-        grid=(steps,),
-        in_specs=[spec] * 4,
-        out_specs=pl.BlockSpec((tiles * 2 * rows, cols), lambda i: (0, 0)),
-        out_shape=jax.ShapeDtypeStruct((tiles * 2 * rows, cols), jnp.float32),
-        scratch_shapes=[
-            pltpu.VMEM((2, tiles * 2 * rows, depth), jnp.bfloat16),
-            pltpu.VMEM((cols, depth), jnp.bfloat16),
-        ],
-        name="bin_pixels",
-    )(*flat)
-    return sums.reshape(tiles, 2, rows, cols)
+GROUPS = 4
+DEPTH = 1024
 
 
 def lane_column(pack, lane, like):
@@ -105,7 +39,10 @@
 
 def apply_kernel(
     counts,
-    sums,
+    fx_ref,
+    fy_ref,
+    tile_ref,
+    cell_ref,
     guess,
     visc,
     fric,
@@ -120,10 +57,17 @@
     bits = nz.bit_length() - 1
     tiles = nx * ny
     layers, rows, cols = visc.shape
+    steps, _, depth = fx_ref.shape
+    groups = GROUPS if tiles % GROUPS == 0 else 1
+    per = tiles // groups
     scratch = list(scratch)
     accs = [scratch.pop(0) for _ in range(bits)]
     recvs = [scratch.pop(0) for _ in range(bits)]
     (
+        sums,
+        lhs,
+        rhs,
+        acc,
         tile_in,
         block,
         forcing,
@@ -190,18 +134,57 @@
     size = rows // nz
     offset = pl.multiple_of(offset, size)
 
-    def half_copy(bit):
+    def half_copy(bit, g):
         _, give, length, peer = starts[bit]
         source = sums if bit == 0 else accs[bit - 1]
+        own = pl.ds(g * per, per)
         return remote(
-            source.at[:, :, pl.ds(give, length), :],
-            recvs[bit],
-            half_sem.at[0, bit],
-            half_sem.at[1, bit],
+            source.at[own, :, pl.ds(give, length), :],
+            recvs[bit].at[own],
+            half_sem.at[0, bit, g],
+            half_sem.at[1, bit, g],
             peer,
         )
 
-    half_copy(0).start()
+    def bin_group(g):
+        acc[...] = jnp.zeros_like(acc)
+
+        def step(i, carry):
+            tile_id = tile_ref[i]
+            cell = cell_ref[i]
+            row = lax.div(cell, cols).astype(jnp.float32)
+            if g == 0:
+                ids = lax.broadcasted_iota(jnp.int32, (cols, depth), 0)
+                ids = ids.astype(jnp.float32).astype(jnp.bfloat16)
+                col = lax.rem(cell, cols).astype(jnp.float32).astype(jnp.bfloat16)
+                one = jnp.ones((cols, depth), jnp.bfloat16)
+                rhs[i] = jnp.where(ids == col, one, jnp.zeros_like(one))
+            pieces = []
+            for value in (fx_ref[i], fy_ref[i]):
+                high = value.astype(jnp.bfloat16)
+                low = (value - high.astype(jnp.float32)).astype(jnp.bfloat16)
+                pieces.append((high, low))
+            ids = lax.broadcasted_iota(jnp.int32, (rows, depth), 0)
+            ids = ids.astype(jnp.float32).astype(jnp.bfloat16)
+            zero = jnp.zeros((rows, depth), jnp.bfloat16)
+            for n in range(per):
+                own = jnp.where(tile_id == g * per + n, row, -1.0).astype(jnp.bfloat16)
+                hit = ids == own
+                for c in range(2):
+                    for part_id in range(2):
+                        start = ((part_id * per + n) * 2 + c) * rows
+                        piece = jnp.broadcast_to(pieces[c][part_id], (rows, depth))
+                        lhs[start : start + rows, :] = jnp.where(hit, piece, zero)
+            acc[...] += lax.dot_general(
+                lhs[...], rhs[i], (((1,), (1,)), ((), ())), preferred_element_type=jnp.float32
+            )
+            return carry
+
+        lax.fori_loop(0, steps, step, 0)
+        half = per * 2 * rows
+        sums[g * per : (g + 1) * per] = (acc[0:half] + acc[half : 2 * half]).reshape(
+            per, 2, rows, cols
+        )
 
     def pack(field):
         lanes = lax.broadcasted_iota(jnp.int32, (rows, 128), 1)
@@ -350,42 +333,75 @@
             low_a, low_b = top_a, top_b
             damp = damping_of(k)
             store(k, va, vb, damp, image_a, image_b)
+            yield k
 
     def store_first(k, va, vb, damp, image_a, image_b):
         middle[0, k] = va - damp * image_a
         middle[1, k] = vb - damp * image_b
 
-    for bit in range(bits):
+    def tile_copy(t):
+        device = (t // ny, t % ny, gz)
+        return remote(
+            total.at[t], tile_in.at[tile], tile_sem.at[0, t], tile_sem.at[1, tile], device
+        )
+
+    def finish(bit, g):
         keep, give, length, _ = starts[bit]
         source = sums if bit == 0 else accs[bit - 1]
-        copy = half_copy(bit)
-        copy.wait_recv()
+        own = pl.ds(g * per, per)
+        half_copy(bit, g).wait_recv()
         if bit + 1 < bits:
             next_keep, next_give, next_length, _ = starts[bit + 1]
             for begin in (next_give, next_keep):
-                accs[bit][:, :, pl.ds(begin, next_length), :] = (
-                    source[:, :, pl.ds(pl.multiple_of(keep + begin, next_length), next_length), :]
-                    + recvs[bit][:, :, pl.ds(begin, next_length), :]
+                accs[bit][own, :, pl.ds(begin, next_length), :] = (
+                    source[own, :, pl.ds(pl.multiple_of(keep + begin, next_length), next_length), :]
+                    + recvs[bit][own, :, pl.ds(begin, next_length), :]
                 )
                 if begin is next_give:
-                    half_copy(bit + 1).start()
+                    half_copy(bit + 1, g).start()
+            return
+        accs[bit][own] = source[own, :, pl.ds(keep, length), :] + recvs[bit][own]
+        for t in range(g * per, (g + 1) * per):
+
+            @pl.when(tile != t)
+            def _(t=t):
+                tile_copy(t).start()
+
+            @pl.when(tile == t)
+            def _(t=t):
+                tile_in[t] = total[t]
+
+    total = accs[bits - 1]
+    first_sweep = None
+    for turn in range(groups + bits):
+        if turn < groups:
+            bin_group(turn)
+            half_copy(0, turn).start()
+        elif turn == groups:
+            wait_all(first)
+            first_sweep = sweep(guess, 0, store_first)
+            for _ in range(2):
+                next(first_sweep, None)
         else:
-            accs[bit][...] = source[:, :, pl.ds(keep, length), :] + recvs[bit][...]
-        if bit == bits - 2 or bits == 1:
-            wait_all(first)
-            sweep(guess, 0, store_first)
-    total = accs[bits - 1]
-
-    def tile_copy(o):
-        other, device = tile_peers[o - 1]
-        return remote(total.at[other], tile_in.at[o - 1], tile_sem.at[0, o - 1], tile_sem.at[1, o - 1], device)
-
-    for o in range(1, tiles):
-        tile_copy(o).start()
-    value = total[tile]
-    for o in range(1, tiles):
-        tile_copy(o).wait_recv()
-        value = value + tile_in[o - 1]
+            for _ in range(2):
+                next(first_sweep, None)
+        for bit in reversed(range(bits)):
+            g = turn - 1 - bit
+            if 0 <= g < groups:
+                finish(bit, g)
+    for _ in first_sweep:
+        pass
+    for t in range(tiles):
+
+        @pl.when(tile != t)
+        def _(t=t):
+            remote(
+                total.at[t], tile_in.at[t], tile_sem.at[0, t], tile_sem.at[1, t], (t // ny, t % ny, gz)
+            ).wait_recv()
+
+    value = tile_in[0]
+    for t in range(1, tiles):
+        value = value + tile_in[t]
     block[...] = value
 
     def row_start(j):
@@ -446,7 +462,8 @@
         else:
             part[1] = part[1] + term
 
-    sweep(middle, 1, store_second)
+    for _ in sweep(middle, 1, store_second):
+        pass
     part[1] = 0.25 * mask_float * part[1]
 
     def part_copy(o):
@@ -469,9 +486,13 @@
     maps_out[...] = value
 
     for bit in range(bits):
-        half_copy(bit).wait_send()
-    for o in range(1, tiles):
-        tile_copy(o).wait_send()
+        for g in range(groups):
+            half_copy(bit, g).wait_send()
+    for t in range(tiles):
+
+        @pl.when(tile != t)
+        def _(t=t):
+            tile_copy(t).wait_send()
 
     @pl.when(gz < nz - 1)
     def _():
@@ -481,19 +502,25 @@
         part_copy(o).wait_send()
 
 
-def apply_twice(sums, guess, visc, fric, base, slope, mask, counts):
+def apply_twice(pixels, guess, visc, fric, base, slope, mask, counts):
     nx, ny, nz = counts
     tiles = nx * ny
     bits = nz.bit_length() - 1
     _, layers, rows, cols = guess.shape
     size = rows // nz
     f32 = jnp.float32
+    groups = GROUPS if tiles % GROUPS == 0 else 1
+    per = tiles // groups
+    per_device = pixels[0].shape[0]
+    depth = min(DEPTH, per_device)
+    steps = per_device // depth
+    flat = [value.reshape(steps, 1, depth) for value in pixels]
     halves = [pltpu.VMEM((tiles, 2, rows >> (bit + 1), cols), f32) for bit in range(bits)]
     vmem = pl.BlockSpec(memory_space=pltpu.VMEM)
     dma = pltpu.SemaphoreType.DMA
     return pl.pallas_call(
         functools.partial(apply_kernel, counts),
-        in_specs=[vmem] * 7,
+        in_specs=[vmem] * 10,
         out_specs=(vmem, vmem),
         out_shape=(
             jax.ShapeDtypeStruct(guess.shape, f32),
@@ -502,7 +529,11 @@
         scratch_shapes=halves
         + halves
         + [
-            pltpu.VMEM((tiles - 1, 2, size, cols), f32),
+            pltpu.VMEM((tiles, 2, rows, cols), f32),
+            pltpu.VMEM((per * 4 * rows, depth), jnp.bfloat16),
+            pltpu.VMEM((steps, cols, depth), jnp.bfloat16),
+            pltpu.VMEM((per * 4 * rows, cols), f32),
+            pltpu.VMEM((tiles, 2, size, cols), f32),
             pltpu.VMEM((2, size, cols), f32),
             pltpu.VMEM((2, rows, cols), f32),
             pltpu.VMEM(guess.shape, f32),
@@ -521,8 +552,8 @@
             pltpu.VMEM((rows, cols), f32),
             pltpu.VMEM((2, rows, cols), f32),
             pltpu.VMEM((nz - 1, 2, size, cols), f32),
-            dma((2, bits)),
-            dma((2, tiles - 1)),
+            dma((2, bits, groups)),
+            dma((2, tiles)),
             dma,
             dma((nz,)),
             dma((2, 2, 8)),
@@ -533,7 +564,7 @@
             collective_id=0, has_side_effects=True, vmem_limit_bytes=56 * 2**20
         ),
         name="apply_twice",
-    )(sums, guess, visc, fric, base, slope, mask)
+    )(*flat, guess, visc, fric, base, slope, mask)
 
 
 def body(
@@ -549,26 +580,20 @@
     pixel_cell,
     pixel_count,
 ):
-    rows_local = adjoint_guess.shape[2]
-    cols_local = adjoint_guess.shape[3]
     count_x = lax.axis_size("gx")
     count_y = lax.axis_size("gy")
     count_z = lax.axis_size("gz")
-    tile_total = count_x * count_y
     per_device = pixel_misfit.shape[0]
     live = jnp.arange(per_device, dtype=jnp.int32) < pixel_count[0]
     values = jnp.where(live, pixel_misfit, jnp.float32(0.0))
-    sums = bin_pixels(
+    pixels = (
         values * jnp.cos(pixel_look),
         values * jnp.sin(pixel_look),
         pixel_tile[:, 0],
         pixel_cell,
-        tile_total,
-        rows_local,
-        cols_local,
     )
     return apply_twice(
-        sums,
+        pixels,
         adjoint_guess,
         viscosity,
         friction,

time: 64.2 us -> 63.8 us (level)
  the two profiles are of different devices: /device:TPU:0 before, /device:TPU:21 now
where the time goes in v3:
time: 63.8 us; the launch traced here: 63.6 us
  Pallas kernels  57.9 us (91%)
  local copies, waits for them, and re-layouts  2.6 us (4%)
  other arithmetic  1.77 us (3%)
  between operations  1.29 us (2%)
    pallas_call x1, Pallas kernels, apply_twice(): pl.pallas_call(functools.partial(apply_kernel, counts), in_specs=[vmem] *...  57.9 us
    unnamed x4, local copies, waits for them, and re-layouts  2.6 us
    mul x1, other arithmetic, body(): values * jnp.sin(pixel_look)  1.77 us

profile of v3, /device:TPU:21, one launch (start us, length us, event | category | flops | bytes accessed | tf_op | source)
XLA Modules:
  0.0 63.6 jit_solution(386188082934546917)
XLA Ops:
  1.3 1.8 %sine_multiply_fusion = (f32[16384]{0:T(1024)}, f32[16384]{0:T(1024)}) fusion(f32[16384]{0:T(1024)} %param.18, f32[16384]{0:T(1024)} %param.17, s32[]{:T(128)} %bitcast.5), kind=kLoop, calls=%fused_computation | loop fusion | flops 65536 | bytes 262148 | tf_op jit(solution)/shard_map/mul | solution.py:591
  3.1 57.9 %apply_twice.1 = (f32[2,5,64,256]{3,2,1,0:T(8,128)}, f32[2,16,256]{2,1,0:T(8,128)}) custom-call(f32[16,1,1024]{2,1,0:T(1,128)} %bitcast.7, f32[16,1,1024]{2,1,0:T(1,128)} %bitcast.6, s32[16,1,1024]{2,1,0:T(1,128)} %bitcast.8, s32[16,1,1024]{2,1,0:T(1,128)} %bitcast.9, f32[2,5,64,256]{3,2,1,0:T(8,128)} %guess.1, f32[5,64,256]{2,1,0:T(8,128)} %visc.1, ...), custom_call_target="tpu_custom_call" | custom-call | tf_op jit(solution)/shard_map/apply_twice/pallas_call | solution.py:521
  61.0 0.0 copy-start
  61.0 2.0 %copy.16 = f32[2,5,64,256]{3,2,1,0:T(8,128)} copy(f32[2,5,64,256]{3,2,1,0:T(8,128)} %get-tuple-element.6) | data formatting | bytes 1310720
  63.0 0.0 copy-done
  63.0 0.6 copy.17
Async XLA Ops:
  61.0 2.0 %copy-start = (f32[2,16,256]{2,1,0:T(8,128)S(1)}, f32[2,16,256]{2,1,0:T(8,128)}, u32[]{:S(2)}) copy-start(f32[2,16,256]{2,1,0:T(8,128)} %get-tuple-element.7) | copy-start | bytes 98308

commit v4 on v3

--- a/solution.py
+++ b/solution.py
@@ -1,4 +1,5 @@
 import functools
+import math
 
 import jax
 import jax.numpy as jnp
@@ -8,6 +9,7 @@
 from jax.sharding import PartitionSpec as P
 
 GROUPS = 4
+SLOT_TILES = 8
 DEPTH = 1024
 
 
@@ -149,7 +151,7 @@
     def bin_group(g):
         acc[...] = jnp.zeros_like(acc)
 
-        def step(i, carry):
+        def step(i, slot):
             tile_id = tile_ref[i]
             cell = cell_ref[i]
             row = lax.div(cell, cols).astype(jnp.float32)
@@ -174,13 +176,18 @@
                     for part_id in range(2):
                         start = ((part_id * per + n) * 2 + c) * rows
                         piece = jnp.broadcast_to(pieces[c][part_id], (rows, depth))
-                        lhs[start : start + rows, :] = jnp.where(hit, piece, zero)
+                        lhs[slot, start : start + rows, :] = jnp.where(hit, piece, zero)
             acc[...] += lax.dot_general(
-                lhs[...], rhs[i], (((1,), (1,)), ((), ())), preferred_element_type=jnp.float32
+                lhs[slot], rhs[i], (((1,), (1,)), ((), ())), preferred_element_type=jnp.float32
             )
+
+        def several(j, carry):
+            for slot in range(unroll):
+                step(j * unroll + slot, slot)
             return carry
 
-        lax.fori_loop(0, steps, step, 0)
+        unroll = lhs.shape[0]
+        lax.fori_loop(0, steps // unroll, several, 0)
         half = per * 2 * rows
         sums[g * per : (g + 1) * per] = (acc[0:half] + acc[half : 2 * half]).reshape(
             per, 2, rows, cols
@@ -515,6 +522,7 @@
     depth = min(DEPTH, per_device)
     steps = per_device // depth
     flat = [value.reshape(steps, 1, depth) for value in pixels]
+    slots = math.gcd(steps, max(1, SLOT_TILES // per))
     halves = [pltpu.VMEM((tiles, 2, rows >> (bit + 1), cols), f32) for bit in range(bits)]
     vmem = pl.BlockSpec(memory_space=pltpu.VMEM)
     dma = pltpu.SemaphoreType.DMA
@@ -530,7 +538,7 @@
         + halves
         + [
             pltpu.VMEM((tiles, 2, rows, cols), f32),
-            pltpu.VMEM((per * 4 * rows, depth), jnp.bfloat16),
+            pltpu.VMEM((slots, per * 4 * rows, depth), jnp.bfloat16),
             pltpu.VMEM((steps, cols, depth), jnp.bfloat16),
             pltpu.VMEM((per * 4 * rows, cols), f32),
             pltpu.VMEM((tiles, 2, size, cols), f32),

time: 63.8 us -> 53.6 us (0.84)
  Pallas kernels: 57.9 us -> 47.7 us
    pallas_call x1, Pallas kernels: 57.9 us -> 47.7 us  [apply_twice(): pl.pallas_call(functools.partial(apply_kernel, counts), in_specs=[vmem] *...]
where the time goes in v4:
time: 53.6 us; the launch traced here: 53.4 us
  Pallas kernels  47.7 us (89%)
  local copies, waits for them, and re-layouts  2.6 us (5%)
  other arithmetic  1.77 us (3%)
  between operations  1.29 us (2%)
    pallas_call x1, Pallas kernels, apply_twice(): pl.pallas_call(functools.partial(apply_kernel, counts), in_specs=[vmem] *...  47.7 us
    unnamed x4, local copies, waits for them, and re-layouts  2.6 us
    mul x1, other arithmetic, body(): values * jnp.sin(pixel_look)  1.77 us

profile of v4, /device:TPU:21, one launch (start us, length us, event | category | flops | bytes accessed | tf_op | source)
XLA Modules:
  0.0 53.4 jit_solution(8745041646859811128)
XLA Ops:
  1.3 1.8 %sine_multiply_fusion = (f32[16384]{0:T(1024)}, f32[16384]{0:T(1024)}) fusion(f32[16384]{0:T(1024)} %param.18, f32[16384]{0:T(1024)} %param.17, s32[]{:T(128)} %bitcast.5), kind=kLoop, calls=%fused_computation | loop fusion | flops 65536 | bytes 262148 | tf_op jit(solution)/shard_map/mul | solution.py:599
  3.1 47.7 %apply_twice.1 = (f32[2,5,64,256]{3,2,1,0:T(8,128)}, f32[2,16,256]{2,1,0:T(8,128)}) custom-call(f32[16,1,1024]{2,1,0:T(1,128)} %bitcast.7, f32[16,1,1024]{2,1,0:T(1,128)} %bitcast.6, s32[16,1,1024]{2,1,0:T(1,128)} %bitcast.8, s32[16,1,1024]{2,1,0:T(1,128)} %bitcast.9, f32[2,5,64,256]{3,2,1,0:T(8,128)} %guess.1, f32[5,64,256]{2,1,0:T(8,128)} %visc.1, ...), custom_call_target="tpu_custom_call" | custom-call | tf_op jit(solution)/shard_map/apply_twice/pallas_call | solution.py:529
  50.8 0.0 copy-start
  50.8 2.0 %copy.16 = f32[2,5,64,256]{3,2,1,0:T(8,128)} copy(f32[2,5,64,256]{3,2,1,0:T(8,128)} %get-tuple-element.6) | data formatting | bytes 1310720
  52.8 0.0 copy-done
  52.8 0.6 %copy.17 = f32[2,16,256]{2,1,0:T(8,128)} copy(f32[2,16,256]{2,1,0:T(8,128)S(1)} %copy-done) | data formatting | bytes 65536
Async XLA Ops:
  50.8 2.0 %copy-start = (f32[2,16,256]{2,1,0:T(8,128)S(1)}, f32[2,16,256]{2,1,0:T(8,128)}, u32[]{:S(2)}) copy-start(f32[2,16,256]{2,1,0:T(8,128)} %get-tuple-element.7) | copy-start | bytes 98308
